TPU v7x, 256 devices: a whole 4x4x8 slice. The times are simulated.
256 devices in a mesh: aa: 8 (over x, core), ba: 32 (over z, y).
Axes of the slice: x: 4, y: 4, z: 8, core: 2. Of those that a mesh axis runs over, the one named last changes fastest.
Arguments:
- tokens: bfloat16 [262144, 2048], P(('aa', 'ba')), may hold values from -42 to 42
- grad_out: bfloat16 [262144, 1024], P(('aa', 'ba')), may hold values from -6 to 6
- master_weight: float32 [2048, 1024], P(('aa', 'ba')), may hold values from -0.003 to 0.003
- first_moment: float32 [2048, 1024], P(('aa', 'ba')), may hold values from -0.6 to 0.6
- second_moment: float32 [2048, 1024], P(('aa', 'ba')), may hold values from 0.02 to 0.2
- next_tokens: bfloat16 [262144, 2048], P(('aa', 'ba')), may hold values from -72 to 72
Outputs:
- new_first: float32 [2048, 1024], P(('aa', 'ba'))
- new_second: float32 [2048, 1024], P(('aa', 'ba'))
- next_hidden: bfloat16 [262144, 512], P(('aa', 'ba'))
All inputs are finite; a program needn't handle non-finite values.
Results may differ from a plain program's by a relative error of at most 0.0064.
Values may be sent and summed in bfloat16 or wider, within the bound.
A program may use at most 64 MiB of HBM per device.

v0:
```python
import functools
import math

import jax
import jax.numpy as jnp
from jax import lax
from jax.sharding import Mesh
from jax.sharding import PartitionSpec as P

D = 2048
FF = 512
QB = 128
AA = ("aa_0", "aa_1")
BA = ("ba_0", "ba_1")
AA_BA = ("aa_0", "aa_1", "ba_0", "ba_1")


def in_one_piece(arrays, axis, split_dim, concat_dim, along):
    widths = [math.prod(a.shape[along:]) for a in arrays]
    both = jnp.concatenate(
        [a.reshape(*a.shape[:along], w) for a, w in zip(arrays, widths)], axis=along
    )
    result = lax.all_to_all(both, axis, split_axis=split_dim, concat_axis=concat_dim, tiled=True)
    pieces = jnp.split(result, [sum(widths[:k]) for k in range(1, len(widths))], axis=along)
    return tuple(
        (b.reshape(*result.shape[:along], *a.shape[along:]) for a, b in zip(arrays, pieces))
    )


def one_axis_at_a_time(value, axes):
    return functools.reduce(lax.psum, axes, value)


def from_everyone(value, axis):
    copies = jnp.broadcast_to(value, (lax.axis_size(axis), *value.shape))
    return lax.all_to_all(copies, axis, split_axis=0, concat_axis=0, tiled=True)


def in_order(pieces, dim):
    shape = list(pieces.shape[1:])
    shape[dim] *= pieces.shape[0]
    return jnp.moveaxis(pieces, 0, dim).reshape(shape)


def gathered_copies(value, axis, dim):
    pieces = from_everyone(value, axis)
    return in_order(pieces, dim)


def encode_blocks(matrix):
    height, width = matrix.shape
    blocks = matrix.reshape(height, width // QB, QB)
    largest = jnp.max(jnp.abs(blocks), axis=2)
    scales = ((largest + 1e-06) / 448.0).astype(jnp.bfloat16)
    codes = (blocks / scales.astype(jnp.float32)[:, :, None]).astype(jnp.bfloat16)
    return (codes, scales)


def decoded_sum(codes, scales):
    values = codes.astype(jnp.float32) * scales.astype(jnp.float32)[:, :, :, None]
    summed = jnp.sum(values, axis=0)
    return summed.reshape(summed.shape[0], summed.shape[1] * summed.shape[2])


def reduce_tensor(tokens, cotangent):
    groups_outer = lax.axis_size(AA)
    groups_inner = lax.axis_size(BA)
    local_grad = lax.dot_general(
        tokens, cotangent, (((0,), (0,)), ((), ())), preferred_element_type=jnp.float32
    )
    height = local_grad.shape[0]
    codes, scales = encode_blocks(local_grad)
    codes = codes.reshape(groups_outer, height // groups_outer, codes.shape[1], codes.shape[2])
    scales = scales.reshape(groups_outer, height // groups_outer, scales.shape[1])
    codes, scales = in_one_piece((codes, scales), AA, 0, 0, 3)
    partial_value = decoded_sum(codes, scales)
    rows_part = partial_value.shape[0]
    codes, scales = encode_blocks(partial_value)
    codes = codes.reshape(groups_inner, rows_part // groups_inner, codes.shape[1], codes.shape[2])
    scales = scales.reshape(groups_inner, rows_part // groups_inner, scales.shape[1])
    codes, scales = in_one_piece((codes, scales), BA, 0, 0, 3)
    return decoded_sum(codes, scales)


def shards(tokens, grad_out, master_weight, first_moment, second_moment, next_tokens):
    half_width = grad_out.shape[1] // 2
    gate_grad = reduce_tensor(tokens, grad_out[:, :half_width])
    up_grad = reduce_tensor(tokens, grad_out[:, half_width:])
    gate_sq, up_sq = (
        one_axis_at_a_time(jnp.sum(gate_grad * gate_grad), AA_BA),
        one_axis_at_a_time(jnp.sum(up_grad * up_grad), AA_BA),
    )
    limit = math.sqrt(D * FF)
    gate_factor = jnp.minimum(1.0, limit / jnp.sqrt(gate_sq + 1e-06))
    up_factor = jnp.minimum(1.0, limit / jnp.sqrt(up_sq + 1e-06))
    clipped = jnp.concatenate([gate_grad * gate_factor, up_grad * up_factor], axis=1)
    new_first = 0.9 * first_moment + 0.1 * clipped
    new_second = 0.95 * second_moment + 0.05 * clipped * clipped
    corr_first = 1.0 - 0.9**10
    corr_second = 1.0 - 0.95**10
    updated = master_weight * (1.0 - 0.003 * 0.1) - 0.003 * (new_first / corr_first) / (
        jnp.sqrt(new_second / corr_second) + 1e-08
    )
    low_weight = updated.astype(jnp.bfloat16)
    block_rows = gathered_copies(low_weight, BA, 0)
    whole_weight = lax.all_gather(block_rows, AA, axis=0, tiled=True)
    projected = jnp.dot(next_tokens, whole_weight, preferred_element_type=jnp.float32)
    next_hidden = (jax.nn.silu(projected[:, :half_width]) * projected[:, half_width:]).astype(
        jnp.bfloat16
    )
    return (new_first, new_second, next_hidden)


def solution(mesh):
    split = Mesh(mesh.devices.reshape(4, 2, 8, 4), ("aa_0", "aa_1", "ba_0", "ba_1"))
    return jax.shard_map(
        shards,
        mesh=split,
        in_specs=(
            P(AA_BA, None),
            P(AA_BA, None),
            P(AA_BA, None),
            P(AA_BA, None),
            P(AA_BA, None),
            P(AA_BA, None),
        ),
        out_specs=(P(AA_BA, None), P(AA_BA, None), P(AA_BA, None)),
        check_vma=False,
    )
```

profile of v0, /device:TPU:1, one launch (start us, length us, event | category | flops | bytes accessed | tf_op | source)
XLA Modules:
  0.0 245.4 jit_solution(15333974454503087429)
XLA Ops:
  7.2 4.9 %bitcast_reduce_fusion = (f32[2048,4]{0,1:T(4,128)S(1)}, f32[2048,512]{0,1:T(8,128)S(1)}) fusion(bf16[1024,2048]{1,0:T(8,128)(2,1)} %param.6, bf16[1024,1024]{1,0:T(8,128)(2,1)} %param.7), kind=kOutput, calls=%fused_computation | convolution fusion | flops 2149572608 | bytes 9469952 | tf_op jit(solution)/shard_map/dot_general | solution.py:68
  12.1 2.0 copy.82
  14.1 2.7 %fusion.1 = bf16[8,256,4,128]{1,2,3,0:T(4,128)(2,1)S(1)} fusion(f32[8,256,4,128]{1,0,3,2:T(8,128)S(1)} %bitcast.64, f32[8,256,4]{1,2,0:T(4,128)S(1)} %convert.11), kind=kLoop, calls=%fused_computation.7 | loop fusion | flops 2097152 | bytes 6324224 | tf_op jit(solution)/shard_map/convert_element_type | solution.py:55
  16.8 2.7 %pad_maximum_fusion.1 = bf16[8,256,4,129]{1,2,3,0:T(4,128)(2,1)} fusion(bf16[8,256,4,1]{1,2,3,0:T(4,128)(2,1)S(1)} %bitcast.69, bf16[8,256,4,128]{1,2,3,0:T(4,128)(2,1)S(1)} %fusion.1), kind=kLoop, calls=%fused_computation.10 | loop fusion | flops 1056768 | bytes 4227072 | tf_op jit(solution)/shard_map/concatenate | solution.py:20
  19.5 6.7 %all-to-all-start.2 = ((bf16[8,256,4,129]{1,2,3,0:T(4,128)(2,1)}), bf16[8,256,4,129]{1,2,3,0:T(4,128)(2,1)S(1)}, u32[]{:S(2)}, u32[]{:S(2)}) async-start(bf16[8,256,4,129]{1,2,3,0:T(4,128)(2,1)} %pad_maximum_fusion.1), calls=%async_computation.2 | async-start | bytes 4227072 | tf_op jit(solution)/shard_map/all_to_all | solution.py:23
  26.2 4.9 %bitcast_reduce_fusion.1 = (f32[2048,4]{0,1:T(4,128)S(1)}, f32[2048,512]{0,1:T(8,128)S(1)}) fusion(bf16[1024,2048]{1,0:T(8,128)(2,1)} %param.6, bf16[1024,1024]{1,0:T(8,128)(2,1)} %param.7), kind=kOutput, calls=%fused_computation.1 | convolution fusion | flops 2149572608 | bytes 9469952 | tf_op jit(solution)/shard_map/dot_general | solution.py:68
  31.1 2.0 copy.81
  33.1 2.7 %fusion = bf16[8,256,4,128]{1,2,3,0:T(4,128)(2,1)S(1)} fusion(f32[8,256,4,128]{1,0,3,2:T(8,128)S(1)} %bitcast.63, f32[8,256,4]{1,2,0:T(4,128)S(1)} %convert.8), kind=kLoop, calls=%fused_computation.6 | loop fusion | flops 2097152 | bytes 6324224 | tf_op jit(solution)/shard_map/convert_element_type | solution.py:55
  35.8 2.7 %pad_maximum_fusion = bf16[8,256,4,129]{1,2,3,0:T(4,128)(2,1)} fusion(bf16[8,256,4,1]{1,2,3,0:T(4,128)(2,1)S(1)} %bitcast.71, bf16[8,256,4,128]{1,2,3,0:T(4,128)(2,1)S(1)} %fusion), kind=kLoop, calls=%fused_computation.9 | loop fusion | flops 1056768 | bytes 4227072 | tf_op jit(solution)/shard_map/concatenate | solution.py:20
  38.5 14.1 %all-to-all-done.2 = bf16[8,256,4,129]{1,2,3,0:T(4,128)(2,1)S(1)} async-done(((bf16[8,256,4,129]{1,2,3,0:T(4,128)(2,1)}), bf16[8,256,4,129]{1,2,3,0:T(4,128)(2,1)S(1)}, u32[]{:S(2)}, u32[]{:S(2)}) %all-to-all-start.2) | async-done | bytes 2113568 | tf_op jit(solution)/shard_map/all_to_all | solution.py:23
  52.6 5.2 %all-to-all-start = ((bf16[8,256,4,129]{1,2,3,0:T(4,128)(2,1)}), bf16[8,256,4,129]{1,2,3,0:T(4,128)(2,1)}, u32[]{:S(2)}, u32[]{:S(2)}) async-start(bf16[8,256,4,129]{1,2,3,0:T(4,128)(2,1)} %pad_maximum_fusion), calls=%async_computation | async-start | bytes 4227072 | tf_op jit(solution)/shard_map/all_to_all | solution.py:23
  57.8 1.2 multiply_reduce_fusion
  59.1 0.2 copy.69
  59.3 0.1 fusion.7
  59.4 0.1 reshape.192
  59.5 0.4 convert_element_type.185
  59.9 24.4 %all-to-all-done = bf16[8,256,4,129]{1,2,3,0:T(4,128)(2,1)} async-done(((bf16[8,256,4,129]{1,2,3,0:T(4,128)(2,1)}), bf16[8,256,4,129]{1,2,3,0:T(4,128)(2,1)}, u32[]{:S(2)}, u32[]{:S(2)}) %all-to-all-start) | async-done | bytes 2113568 | tf_op jit(solution)/shard_map/all_to_all | solution.py:23
  84.3 0.7 fusion.13
  85.1 2.9 %multiply_reduce_fusion.1 = f32[256,4,128]{0,1,2:T(4,128)S(1)} fusion(bf16[8,256,4,129]{1,2,3,0:T(4,128)(2,1)} %all-to-all-done, f32[8,256,4]{1,2,0:T(4,128)S(1)} %fusion.13), kind=kLoop, calls=%fused_computation.5 | loop fusion | flops 3014656 | bytes 2654208 | tf_op jit(solution)/shard_map/reduce_sum | solution.py:61
  88.0 0.1 fusion.8
  88.1 0.2 copy.60
  88.3 0.2 fusion.9
  88.5 0.1 pad_maximum_fusion.3
  88.6 0.9 copy.71
  89.5 10.4 %all-to-all-start.3 = ((bf16[32,8,4,129]{3,1,2,0:T(8,128)(2,1)}), bf16[32,8,4,129]{3,1,2,0:T(8,128)(2,1)S(1)}, u32[]{:S(2)}, u32[]{:S(2)}) async-start(bf16[32,8,4,129]{3,1,2,0:T(8,128)(2,1)} %copy.71), calls=%async_computation.3 | async-start | bytes 1048576 | tf_op jit(solution)/shard_map/all_to_all | solution.py:23
  100.0 0.4 convert_element_type.184
  100.4 0.2 fusion.10
  100.7 0.1 pad_maximum_fusion.2
  100.8 0.9 copy.62
  101.6 13.6 %all-to-all-done.3 = bf16[32,8,4,129]{3,1,2,0:T(8,128)(2,1)S(1)} async-done(((bf16[32,8,4,129]{3,1,2,0:T(8,128)(2,1)}), bf16[32,8,4,129]{3,1,2,0:T(8,128)(2,1)S(1)}, u32[]{:S(2)}, u32[]{:S(2)}) %all-to-all-start.3) | async-done | bytes 264224 | tf_op jit(solution)/shard_map/all_to_all | solution.py:23
  115.3 6.2 %all-to-all-start.1 = ((bf16[32,8,4,129]{3,1,2,0:T(8,128)(2,1)}), bf16[32,8,4,129]{3,1,2,0:T(8,128)(2,1)S(1)}, u32[]{:S(2)}, u32[]{:S(2)}) async-start(bf16[32,8,4,129]{3,1,2,0:T(8,128)(2,1)} %copy.62), calls=%async_computation.1 | async-start | bytes 1048576 | tf_op jit(solution)/shard_map/all_to_all | solution.py:23
  121.5 0.4 copy.78
  122.0 0.2 multiply_reduce_fusion.2
  122.2 0.6 multiply_reduce_fusion.4
  122.8 13.8 %all-to-all-done.1 = bf16[32,8,4,129]{3,1,2,0:T(8,128)(2,1)S(1)} async-done(((bf16[32,8,4,129]{3,1,2,0:T(8,128)(2,1)}), bf16[32,8,4,129]{3,1,2,0:T(8,128)(2,1)S(1)}, u32[]{:S(2)}, u32[]{:S(2)}) %all-to-all-start.1) | async-done | bytes 264224 | tf_op jit(solution)/shard_map/all_to_all | solution.py:23
  136.7 0.4 copy.77
  137.2 0.2 multiply_reduce_fusion.3
  137.4 0.6 multiply_reduce_fusion.5
  138.0 7.5 %all-reduce.2 = (f32[]{:T(128)}, f32[]{:T(128)}) all-reduce(f32[]{:T(128)} %multiply_reduce_fusion.4, f32[]{:T(128)} %multiply_reduce_fusion.5), channel_id=1, replica_groups=mesh['aa_0'=4,'aa_1'=2,'ba_0'=8,'ba_1'=4] {'aa_0'}, use_global_device_ids=true, to_apply=%region_14.0 | all-reduce | flops 2 | bytes 16 | tf_op jit(solution)/shard_map/psum | solution.py:31
  145.5 8.3 %all-reduce.3 = (f32[]{:T(128)}, f32[]{:T(128)}) all-reduce(f32[]{:T(128)} %get-tuple-element.25, f32[]{:T(128)} %get-tuple-element.26), channel_id=1, replica_groups=mesh['aa_0'=4,'aa_1'=2,'ba_0'=8,'ba_1'=4] {'aa_1'}, use_global_device_ids=true, to_apply=%region_15.0 | all-reduce | flops 2 | bytes 16 | tf_op jit(solution)/shard_map/psum | solution.py:31
  153.8 12.3 %all-reduce = (f32[]{:T(128)}, f32[]{:T(128)}) all-reduce(f32[]{:T(128)} %get-tuple-element.27, f32[]{:T(128)} %get-tuple-element.28), channel_id=1, replica_groups=mesh['aa_0'=4,'aa_1'=2,'ba_0'=8,'ba_1'=4] {'ba_0'}, use_global_device_ids=true, to_apply=%region_16.0 | all-reduce | flops 2 | bytes 16 | tf_op jit(solution)/shard_map/psum | solution.py:31
  166.1 7.6 %all-reduce.1 = (f32[]{:T(128)}, f32[]{:T(128)}) all-reduce(f32[]{:T(128)} %get-tuple-element.21, f32[]{:T(128)} %get-tuple-element.22), channel_id=1, replica_groups=mesh['aa_0'=4,'aa_1'=2,'ba_0'=8,'ba_1'=4] {'ba_1'}, use_global_device_ids=true, to_apply=%region_17.0 | all-reduce | flops 2 | bytes 16 | tf_op jit(solution)/shard_map/psum | solution.py:31
  175.2 0.6 subtract_convert_fusion
  175.9 17.7 %all_to_all.25 = bf16[32,8,1024]{2,1,0:T(8,128)(2,1)} all-to-all(bf16[32,8,1024]{2,1,0:T(8,128)(2,1)S(1)} %broadcast_in_dim.2), channel_id=1, replica_groups=mesh['aa_0'=4,'aa_1'=2,'ba_0'=8,'ba_1'=4] {'ba_0','ba_1'}, dimensions={0} | all-to-all | bytes 1048576 | tf_op jit(solution)/shard_map/all_to_all | solution.py:36
  193.6 35.4 %all-gather.2.cloned.1.call-done = bf16[2048,1024]{1,0:T(8,128)(2,1)} async-done(((bf16[256,1024]{1,0:T(8,128)(2,1)}), bf16[2048,1024]{1,0:T(8,128)(2,1)}) %all-gather.2.cloned.1.call-update) | async-done | bytes 4194320 | tf_op jit(solution)/shard_map/all_gather | solution.py:106
  228.9 7.6 %convolution_bitcast_fusion = f32[1024,1024]{0,1:T(8,128)S(1)} fusion(bf16[2048,1024]{1,0:T(8,128)(2,1)} %all-gather.2.cloned.1.call-done, bf16[1024,2048]{1,0:T(8,128)(2,1)} %param.11), kind=kOutput, calls=%fused_computation.8 | convolution fusion | flops 4294967296 | bytes 12582912 | tf_op jit(solution)/shard_map/dot_general | solution.py:107
  236.6 0.6 fusion.2
  237.2 1.3 copy.74
  (24 shorter events, 0.6 us)
Async XLA Ops:
  19.5 33.1 %all-to-all-start.2 = ((bf16[8,256,4,129]{1,2,3,0:T(4,128)(2,1)}), bf16[8,256,4,129]{1,2,3,0:T(4,128)(2,1)S(1)}, u32[]{:S(2)}, u32[]{:S(2)}) async-start(bf16[8,256,4,129]{1,2,3,0:T(4,128)(2,1)} %pad_maximum_fusion.1), calls=%async_computation.2 | async-start | bytes 4227072 | tf_op jit(solution)/shard_map/all_to_all | solution.py:23
  52.6 31.7 %all-to-all-start = ((bf16[8,256,4,129]{1,2,3,0:T(4,128)(2,1)}), bf16[8,256,4,129]{1,2,3,0:T(4,128)(2,1)}, u32[]{:S(2)}, u32[]{:S(2)}) async-start(bf16[8,256,4,129]{1,2,3,0:T(4,128)(2,1)} %pad_maximum_fusion), calls=%async_computation | async-start | bytes 4227072 | tf_op jit(solution)/shard_map/all_to_all | solution.py:23
  89.5 85.7 %copy-start = (f32[8,1024]{1,0:T(8,128)S(1)}, f32[8,1024]{1,0:T(8,128)}, u32[]{:S(2)}) copy-start(f32[8,1024]{1,0:T(8,128)} %param.8) | copy-start | bytes 98308
  89.5 85.7 %copy-start.1 = (f32[8,1024]{1,0:T(8,128)S(1)}, f32[8,1024]{1,0:T(8,128)}, u32[]{:S(2)}) copy-start(f32[8,1024]{1,0:T(8,128)} %param.10) | copy-start | bytes 98308
  89.5 85.7 %copy-start.2 = (f32[8,1024]{1,0:T(8,128)S(1)}, f32[8,1024]{1,0:T(8,128)}, u32[]{:S(2)}) copy-start(f32[8,1024]{1,0:T(8,128)} %param.9) | copy-start | bytes 98308
  89.5 25.8 %all-to-all-start.3 = ((bf16[32,8,4,129]{3,1,2,0:T(8,128)(2,1)}), bf16[32,8,4,129]{3,1,2,0:T(8,128)(2,1)S(1)}, u32[]{:S(2)}, u32[]{:S(2)}) async-start(bf16[32,8,4,129]{3,1,2,0:T(8,128)(2,1)} %copy.71), calls=%async_computation.3 | async-start | bytes 1048576 | tf_op jit(solution)/shard_map/all_to_all | solution.py:23
  115.3 21.4 %all-to-all-start.1 = ((bf16[32,8,4,129]{3,1,2,0:T(8,128)(2,1)}), bf16[32,8,4,129]{3,1,2,0:T(8,128)(2,1)S(1)}, u32[]{:S(2)}, u32[]{:S(2)}) async-start(bf16[32,8,4,129]{3,1,2,0:T(8,128)(2,1)} %copy.62), calls=%async_computation.1 | async-start | bytes 1048576 | tf_op jit(solution)/shard_map/all_to_all | solution.py:23
  121.4 107.5 %all-gather.2.cloned.1.call-start = ((), (), s32[]{:S(2)}) async-start(), calls=%async_computation.5 | async-start | bytes 4718592 | tf_op jit(solution)/shard_map/all_gather | solution.py:106
Sparse Core Ops, SparseCore 0:
  193.7 35.2 all-gather.1
where the time goes:
time: 246 us; the launch traced here: 245 us
  waiting for transfers between devices  101 us (41%)
  blocking collectives  53.4 us (22%)
  starting transfers between devices  28.5 us (12%)
  other arithmetic  19.5 us (8%)
  matrix products  17.4 us (7%)
  between operations  15.7 us (6%)
  local copies, waits for them, and re-layouts  9.55 us (4%)
    all_to_all x4, waiting for transfers between devices, in_one_piece(): lax.all_to_all(both, axis, split_axis=split_dim, concat_axis=concat_dim,...  65.9 us
    psum x4, blocking collectives, one_axis_at_a_time(): return functools.reduce(lax.psum, axes, value)  35.7 us
    all_gather x1, waiting for transfers between devices, shards(): whole_weight = lax.all_gather(block_rows, AA, axis=0, tiled=True)  35.4 us
    all_to_all x4, starting transfers between devices, in_one_piece(): lax.all_to_all(both, axis, split_axis=split_dim, concat_axis=concat_dim,...  28.5 us
    all_to_all x1, blocking collectives, from_everyone(): return lax.all_to_all(copies, axis, split_axis=0, concat_axis=0, tiled=True)  17.7 us
    dot_general x2, matrix products, reduce_tensor(): lax.dot_general(tokens, cotangent, (((0,), (0,)), ((), ())), preferred_el...  9.83 us
    dot_general x1, matrix products, shards(): jnp.dot(next_tokens, whole_weight, preferred_element_type=jnp.float32)  7.61 us
    unnamed x11, local copies, waits for them, and re-layouts  6.01 us
  transfers between devices with their start and end apart: 5, of which 5 were waited for; matrix products, arithmetic and copies ran while one was open for 7% of the time, Pallas kernels for 0%

commit v1 on v0

v1 whole, which is shorter than its diff:
```python
import functools
import math

import jax
import jax.numpy as jnp
from jax import lax
from jax.experimental import pallas as pl
from jax.experimental.pallas import tpu as pltpu
from jax.sharding import Mesh
from jax.sharding import PartitionSpec as P

NX, NC, NZ, NY = 4, 2, 8, 4
ROWS = 8
D = 2048
FF = 512
TOK = 1024
AXES = ("x", "c", "z", "y")
MESH = pl.DeviceIdType.MESH
f32 = jnp.float32
bf16 = jnp.bfloat16


def body(
    tok_hbm, cot_hbm, w_ref, m_ref, v_ref, nxt_hbm,
    nf_ref, nv_ref, out_ref,
    tok, cot, nxt, own, give, take,
    sa, sb, ra1, rb1, ta, tb, ra2, rb2, tz, rz, sq, rsq_z, rsq_y, rsq_x, rsq_c,
    wz, rwz, wa, wb,
    ld, core_s, core_r, a1_s, a1_r, b1_s, b1_r, a2_s, a2_r, b2_s, b2_r, z_s, z_r,
    qz_s, qz_r, qy_s, qy_r, qx_s, qx_r, qc_s, qc_r,
    gz_s, gz_r, ga2_s, ga2_r, gb2_s, gb2_r, ga3_s, ga3_r, gb3_s, gb3_r, gca_s, gca_r, gcb_s, gcb_r,
):
    x, c, z, y = (lax.axis_index(a) for a in AXES)
    other = 1 - c

    def xp(o):
        return {"x": lax.rem(x + o, NX)}

    def yp(o):
        return {"y": lax.rem(y + o, NY)}

    def zp(o):
        return {"z": lax.rem(z + o, NZ)}

    mate = {"c": other}
    peers = [mate] + [xp(o) for o in range(1, NX)] + [yp(o) for o in range(1, NY)] + [zp(o) for o in range(1, NZ)]

    def send(src, dst, ss, rs, to):
        cp = pltpu.make_async_remote_copy(
            src_ref=src, dst_ref=dst, send_sem=ss, recv_sem=rs, device_id=to, device_id_type=MESH
        )
        cp.start()
        return cp

    barrier = pltpu.get_barrier_semaphore()
    for p in peers:
        pl.semaphore_signal(barrier, inc=1, device_id=p, device_id_type=MESH)

    loads = [
        pltpu.make_async_copy(cot_hbm, cot, ld.at[0]),
        pltpu.make_async_copy(tok_hbm, tok, ld.at[1]),
        pltpu.make_async_copy(nxt_hbm, nxt, ld.at[2]),
    ]
    for cp in loads:
        cp.start()
    loads[0].wait()
    loads[1].wait()

    offs = (2, 1, 3, 0)
    blocks = [lax.rem(x + o, NX) for o in offs]

    def block_grad(xb, cc):
        start = pl.multiple_of(xb * 512 + cc * 256, 256)
        return lax.dot_general(
            tok[:, pl.ds(start, 256)], cot[...], (((0,), (0,)), ((), ())), preferred_element_type=f32
        )

    pending = []
    core = []
    for j in range(NX):
        xb = blocks[j]
        give[j] = block_grad(xb, other).astype(bf16).reshape(NZ, NY, ROWS, 2 * FF)
        if j == 0:
            pl.semaphore_wait(barrier, len(peers))
        core.append(send(give.at[j], take.at[j], core_s.at[j], core_r.at[j], mate))
        own[j] = block_grad(xb, c).reshape(NZ, NY, ROWS, 2 * FF)

    a1, b1 = [], []
    for j in range(NX):
        xb, o = blocks[j], offs[j]
        core[j].wait()
        total = own[j] + take[j].astype(f32)
        sa[j] = total[:, :, :, :FF].astype(bf16)
        half = total[:, :, :, FF:].astype(bf16)
        for k in range(NY):
            sb[k, xb] = half[:, k]
        if o:
            a1.append(send(sa.at[j], ra1.at[o - 1], a1_s.at[o - 1], a1_r.at[o - 1], xp(o)))
        for k in range(1, NY):
            yk = lax.rem(y + k, NY)
            b1.append(send(sb.at[yk, xb], rb1.at[k - 1, xb], b1_s.at[k - 1, j], b1_r.at[k - 1, j], yp(k)))
    for cp in a1 + b1:
        cp.wait()

    total = sa[NX - 1].astype(f32)
    for k in range(NX - 1):
        total += ra1[k].astype(f32)
    total = total.astype(bf16)
    for k in range(NY):
        ta[k] = total[:, k]
    for i in range(NX):
        total = sb[y, i].astype(f32)
        for k in range(NY - 1):
            total += rb1[k, i].astype(f32)
        tb[i] = total.astype(bf16)

    st2 = []
    for o in range(1, NY):
        st2.append(send(ta.at[lax.rem(y + o, NY)], ra2.at[o - 1], a2_s.at[o - 1], a2_r.at[o - 1], yp(o)))
        st2.append(send(tb.at[lax.rem(x + o, NX)], rb2.at[o - 1], b2_s.at[o - 1], b2_r.at[o - 1], xp(o)))
    for cp in st2:
        cp.wait()
    total = ta[y].astype(f32)
    for k in range(NY - 1):
        total += ra2[k].astype(f32)
    tz[:, :, :FF] = total.astype(bf16)
    total = tb[x].astype(f32)
    for k in range(NX - 1):
        total += rb2[k].astype(f32)
    tz[:, :, FF:] = total.astype(bf16)

    st3 = []
    for o in range(1, NZ):
        st3.append(send(tz.at[lax.rem(z + o, NZ)], rz.at[o - 1], z_s.at[o - 1], z_r.at[o - 1], zp(o)))
    for cp in st3:
        cp.wait()
    grad = tz[z].astype(f32)
    for k in range(NZ - 1):
        grad += rz[k].astype(f32)

    def fold(t):
        t = t * t
        t = jnp.sum(t, axis=0, keepdims=True)
        return t[:, 0:128] + t[:, 128:256] + t[:, 256:384] + t[:, 384:512]

    def everyone(stage, slots, ss, rs, peer, n):
        cps = [send(sq.at[stage], slots.at[o - 1], ss.at[o - 1], rs.at[o - 1], peer(o)) for o in range(1, n)]
        for cp in cps:
            cp.wait()
        t = sq[stage]
        for k in range(n - 1):
            t = t + slots[k]
        return t

    sq[0] = jnp.concatenate([fold(grad[:, :FF]), fold(grad[:, FF:])], axis=0)
    sq[1] = everyone(0, rsq_z, qz_s, qz_r, zp, NZ)
    sq[2] = everyone(1, rsq_y, qy_s, qy_r, yp, NY)
    sq[3] = everyone(2, rsq_x, qx_s, qx_r, xp, NX)
    both = everyone(3, rsq_c, qc_s, qc_r, lambda o: mate, NC)
    limit = math.sqrt(D * FF)
    factor = jnp.minimum(1.0, limit / jnp.sqrt(jnp.sum(both, axis=1, keepdims=True) + 1e-06))
    gate_factor, up_factor = factor[0:1], factor[1:2]
    clipped = jnp.concatenate([grad[:, :FF] * gate_factor, grad[:, FF:] * up_factor], axis=1)
    new_first = 0.9 * m_ref[...] + 0.1 * clipped
    new_second = 0.95 * v_ref[...] + 0.05 * clipped * clipped
    nf_ref[...] = new_first
    nv_ref[...] = new_second
    corr_first = 1.0 - 0.9**10
    corr_second = 1.0 - 0.95**10
    updated = w_ref[...] * (1.0 - 0.003 * 0.1) - 0.003 * (new_first / corr_first) / (
        jnp.sqrt(new_second / corr_second) + 1e-08
    )
    wz[...] = updated.astype(bf16)

    cps = [send(wz, rwz.at[z], gz_s.at[o - 1], gz_r.at[o - 1], zp(o)) for o in range(1, NZ)]
    rwz[z] = wz[...]
    for cp in cps:
        cp.wait()
    wa[x, c, :, y] = rwz[:, :, :FF]
    wb[x, c, :, y] = rwz[:, :, FF:]
    g2 = []
    for o in range(1, NY):
        g2.append(send(wa.at[x, c, :, y], wa.at[x, c, :, y], ga2_s.at[o - 1], ga2_r.at[o - 1], yp(o)))
        g2.append(send(wb.at[x, c, :, y], wb.at[x, c, :, y], gb2_s.at[o - 1], gb2_r.at[o - 1], xp(o)))
    for cp in g2:
        cp.wait()
    g3 = []
    last = []
    for o in (2, 1, 3):
        g3.append((o, send(wa.at[x, c], wa.at[x, c], ga3_s.at[o - 1], ga3_r.at[o - 1], xp(o)),
                   send(wb.at[:, c, :, y], wb.at[:, c, :, y], gb3_s.at[o - 1], gb3_r.at[o - 1], yp(o))))
    last.append(send(wa.at[x, c], wa.at[x, c], gca_s.at[0], gca_r.at[0], mate))
    last.append(send(wb.at[:, c, :, y], wb.at[:, c, :, y], gcb_s.at[0], gcb_r.at[0], mate))
    for o, ca, cb in (g3[1], g3[2], g3[0]):
        ca.wait()
        xs = lax.rem(x - o + NX, NX)
        last.append(send(wa.at[xs, c], wa.at[xs, c], gca_s.at[o], gca_r.at[o], mate))
        cb.wait()
        ys = lax.rem(y - o + NY, NY)
        last.append(send(wb.at[:, c, :, ys], wb.at[:, c, :, ys], gcb_s.at[o], gcb_r.at[o], mate))
    loads[2].wait()
    for cp in last:
        cp.wait()

    wa2, wb2 = wa.reshape(D, FF), wb.reshape(D, FF)

    def tile(i, _):
        r = pl.ds(pl.multiple_of(i * 256, 256), 256)
        gate = jnp.dot(nxt[r, :], wa2[...], preferred_element_type=f32)
        up = jnp.dot(nxt[r, :], wb2[...], preferred_element_type=f32)
        out_ref[r, :] = (gate / (1.0 + jnp.exp(-gate)) * up).astype(bf16)
        return 0

    lax.fori_loop(0, TOK // 256, tile, 0)


def shards(tokens, grad_out, master_weight, first_moment, second_moment, next_tokens):
    any_ = pl.BlockSpec(memory_space=pl.ANY)
    vm = pl.BlockSpec(memory_space=pltpu.VMEM)
    V = pltpu.VMEM
    dma = pltpu.SemaphoreType.DMA

    def pair(*shape):
        return [dma(shape), dma(shape)]

    scratch = [
        V((TOK, D), bf16), V((TOK, 2 * FF), bf16), V((TOK, D), bf16),
        V((NX, NZ, NY, ROWS, 2 * FF), f32), V((NX, NZ, NY, ROWS, 2 * FF), bf16), V((NX, NZ, NY, ROWS, 2 * FF), bf16),
        V((NX, NZ, NY, ROWS, FF), bf16), V((NY, NX, NZ, ROWS, FF), bf16),
        V((NX - 1, NZ, NY, ROWS, FF), bf16), V((NY - 1, NX, NZ, ROWS, FF), bf16),
        V((NY, NZ, ROWS, FF), bf16), V((NX, NZ, ROWS, FF), bf16),
        V((NY - 1, NZ, ROWS, FF), bf16), V((NX - 1, NZ, ROWS, FF), bf16),
        V((NZ, ROWS, 2 * FF), bf16), V((NZ - 1, ROWS, 2 * FF), bf16),
        V((4, 2, 128), f32), V((NZ - 1, 2, 128), f32), V((NY - 1, 2, 128), f32), V((NX - 1, 2, 128), f32), V((1, 2, 128), f32),
        V((ROWS, 2 * FF), bf16), V((NZ, ROWS, 2 * FF), bf16),
        V((NX, NC, NZ, NY, ROWS, FF), bf16), V((NX, NC, NZ, NY, ROWS, FF), bf16),
        dma((3,)),
        *pair(NX), *pair(NX - 1), *pair(NY - 1, NX), *pair(NY - 1), *pair(NX - 1), *pair(NZ - 1),
        *pair(NZ - 1), *pair(NY - 1), *pair(NX - 1), *pair(1),
        *pair(NZ - 1), *pair(NY - 1), *pair(NX - 1), *pair(NX - 1), *pair(NY - 1), *pair(NX), *pair(NY),
    ]
    return pl.pallas_call(
        body,
        out_shape=(
            jax.ShapeDtypeStruct((ROWS, 2 * FF), f32),
            jax.ShapeDtypeStruct((ROWS, 2 * FF), f32),
            jax.ShapeDtypeStruct((TOK, FF), bf16),
        ),
        in_specs=[any_, any_, vm, vm, vm, any_],
        out_specs=(vm, vm, vm),
        scratch_shapes=scratch,
        compiler_params=pltpu.CompilerParams(
            collective_id=0, has_side_effects=True, vmem_limit_bytes=60 * 1024 * 1024
        ),
    )(tokens, grad_out, master_weight, first_moment, second_moment, next_tokens)


def solution(mesh):
    split = Mesh(mesh.devices.reshape(NX, NC, NZ, NY), AXES)
    rows = P(AXES, None)
    return jax.shard_map(
        shards, mesh=split, in_specs=(rows,) * 6, out_specs=(rows,) * 3, check_vma=False
    )
```

time: 246 us -> 94.5 us (0.38)
  waiting for transfers between devices: 101 us -> 0 us
  Pallas kernels: 0 us -> 88.6 us
  blocking collectives: 53.4 us -> 0 us
  starting transfers between devices: 28.5 us -> 0 us
  other arithmetic: 19.5 us -> 0 us
  matrix products: 17.4 us -> 0 us
  between operations: 15.7 us -> 0.64 us
  local copies, waits for them, and re-layouts: 9.55 us -> 5.01 us
    pallas_call x0 -> x1, Pallas kernels: none -> 88.6 us  [shards(): pl.pallas_call(body, out_shape=(jax.ShapeDtypeStruct((ROWS, 2 * FF), f32)...]
    all_to_all x4 -> x0, waiting for transfers between devices: 65.9 us -> none  [in_one_piece(): lax.all_to_all(both, axis, split_axis=split_dim, concat_axis=concat_dim,...]
    psum x4 -> x0, blocking collectives: 35.7 us -> none  [one_axis_at_a_time(): return functools.reduce(lax.psum, axes, value)]
    all_gather x1 -> x0, waiting for transfers between devices: 35.4 us -> none  [shards(): whole_weight = lax.all_gather(block_rows, AA, axis=0, tiled=True)]
    all_to_all x4 -> x0, starting transfers between devices: 28.5 us -> none  [in_one_piece(): lax.all_to_all(both, axis, split_axis=split_dim, concat_axis=concat_dim,...]
    all_to_all x1 -> x0, blocking collectives: 17.7 us -> none  [from_everyone(): return lax.all_to_all(copies, axis, split_axis=0, concat_axis=0, tiled=True)]
    dot_general x3 -> x0, matrix products: 17.4 us -> none  [the longest x2 9.83 us: reduce_tensor(): lax.dot_general(tokens, cotangent, (((0,), (0,)), ((), ())), preferred_el...]
    convert_element_type x12 -> x0, other arithmetic: 7.17 us -> none  [the longest x4 5.83 us: encode_blocks(): (blocks / scales.astype(jnp.float32)[:, :, None]).astype(jnp.bfloat16)]
  transfers between devices with their start and end apart: 5 -> 0, of which waited for: 5 -> 0; matrix products, arithmetic and copies ran while one was open for 7% -> 0% of each run, Pallas kernels for 0% -> 0%
where the time goes in v1:
time: 94.5 us; the launch traced here: 94.2 us
  Pallas kernels  88.6 us (94%)
  local copies, waits for them, and re-layouts  5.01 us (5%)
    pallas_call x1, Pallas kernels, shards(): pl.pallas_call(body, out_shape=(jax.ShapeDtypeStruct((ROWS, 2 * FF), f32)...  88.6 us
    unnamed x3, local copies, waits for them, and re-layouts  5.01 us

profile of v1, /device:TPU:1, one launch (start us, length us, event | category | flops | bytes accessed | tf_op | source)
XLA Modules:
  0.0 94.2 jit_solution(8663456677556277832)
XLA Ops:
  0.6 88.6 %shard_map.85 = (f32[8,1024]{1,0:T(8,128)}, f32[8,1024]{1,0:T(8,128)}, bf16[1024,512]{1,0:T(8,128)(2,1)}) custom-call(bf16[1024,2048]{1,0:T(8,128)(2,1)} %tok_hbm.1, bf16[1024,1024]{1,0:T(8,128)(2,1)} %cot_hbm.1, f32[8,1024]{1,0:T(8,128)} %w_ref.1, f32[8,1024]{1,0:T(8,128)} %m_ref.1, f32[8,1024]{1,0:T(8,128)} %v_ref.1, bf16[1024,2048]{1,0:T(8,128)(2,1)} %nxt_hbm.1), custom_call_target="tpu_custom_call" | custom-call | tf_op jit(solution)/shard_map/pallas_call | solution.py:242
  89.2 1.4 %copy.12 = f32[8,1024]{1,0:T(8,128)} copy(f32[8,1024]{1,0:T(8,128)} %get-tuple-element.6) | data formatting | bytes 65536
  90.6 1.4 %copy.13 = f32[8,1024]{1,0:T(8,128)} copy(f32[8,1024]{1,0:T(8,128)} %get-tuple-element.7) | data formatting | bytes 65536
  92.0 2.3 %copy.14 = bf16[1024,512]{1,0:T(8,128)(2,1)} copy(bf16[1024,512]{1,0:T(8,128)(2,1)} %get-tuple-element.8) | data formatting | bytes 2097152

commit v2 on v0

v2 whole, which is shorter than its diff:
```python
import math

import jax
import jax.numpy as jnp
from jax import lax
from jax.experimental import pallas as pl
from jax.experimental.pallas import tpu as pltpu
from jax.sharding import Mesh
from jax.sharding import PartitionSpec as P

NX, NC, NZ, NY = 4, 2, 8, 4
ROWS = 8
D = 2048
FF = 512
TOK = 1024
AXES = ("x", "c", "z", "y")
MESH = pl.DeviceIdType.MESH
FAR = (2, 1, 3)
FAR_Z = (4, 3, 5, 2, 6, 1, 7)
f32 = jnp.float32
bf16 = jnp.bfloat16


def body(
    tok_hbm, cot_hbm, w_hbm, m_hbm, v_hbm, nxt_hbm,
    nf_hbm, nv_hbm, out_hbm,
    tok, cot, nxt, pw, own, give, take,
    sa, sb, ra1, rb1, ta, tb, ra2, rb2, tz, rz, sqz, rsqz, rsq, gz, wa, wb, gate_acc, up_acc, nfv, out,
    ld_t, ld_n, ld, core_s, core_r, a1_s, a1_r, b1_s, b1_r, a2_s, a2_r, b2_s, b2_r, z_s, z_r,
    pw_s, pw_r, qz_s, qz_r, q_s, q_r, g_s, g_r,
    ga_s, ga_r, gb_s, gb_r, ha_s, ha_r, hb_s, hb_r, ca_s, ca_r, cb_s, cb_r, st,
):
    x, c, z, y = (lax.axis_index(a) for a in AXES)
    other = 1 - c

    def at_x(o):
        return lax.rem(x + o, NX)

    def at_y(o):
        return lax.rem(y + o, NY)

    def at_z(o):
        return lax.rem(z + o, NZ)

    def xp(o):
        return {"x": at_x(o)}

    def yp(o):
        return {"y": at_y(o)}

    def zp(o):
        return {"z": at_z(o)}

    mate = {"c": other}
    plane = [
        (ox, oc, oy) for ox in (2, 1, 3, 0) for oy in (2, 1, 3, 0) for oc in (1, 0) if ox or oc or oy
    ]

    def in_plane(ox, oc, oy):
        return {"x": at_x(ox), "c": other if oc else c, "y": at_y(oy)}

    sent = []

    def send(src, dst, ss, rs, to):
        cp = pltpu.make_async_remote_copy(
            src_ref=src, dst_ref=dst, send_sem=ss, recv_sem=rs, device_id=to, device_id_type=MESH
        )
        cp.start()
        sent.append(cp)
        return cp

    def arrived(dst, rs):
        pltpu.make_async_remote_copy(
            src_ref=dst, dst_ref=dst, send_sem=rs, recv_sem=rs, device_id=mate, device_id_type=MESH
        ).wait_recv()

    barrier = pltpu.get_barrier_semaphore()
    for o in plane:
        pl.semaphore_signal(barrier, inc=1, device_id=in_plane(*o), device_id_type=MESH)
    for o in FAR_Z:
        pl.semaphore_signal(barrier, inc=1, device_id=zp(o), device_id_type=MESH)

    offs = (2, 1, 3, 0)
    blocks = [at_x(o) for o in offs]
    load_cot = pltpu.make_async_copy(cot_hbm, cot, ld.at[0])
    load_tok = []
    for j in range(NX):
        for i, cc in enumerate((other, c)):
            start = pl.multiple_of(blocks[j] * 512 + cc * 256, 256)
            load_tok.append(
                pltpu.make_async_copy(tok_hbm.at[:, pl.ds(start, 256)], tok.at[2 * j + i], ld_t.at[2 * j + i])
            )
    load_pw = [
        pltpu.make_async_copy(h, pw.at[i, z], ld.at[1 + i]) for i, h in enumerate((w_hbm, m_hbm, v_hbm))
    ]
    load_nxt = [
        pltpu.make_async_copy(nxt_hbm.at[:, pl.ds(k * 512, 512)], nxt.at[k], ld_n.at[k]) for k in range(NX)
    ]
    for cp in [load_tok[0], load_cot, load_tok[1]]:
        cp.start()
    load_cot.wait()
    load_tok[0].wait()
    for cp in load_tok[2:] + load_pw:
        cp.start()

    def block_grad(i):
        if i:
            load_tok[i].wait()
        return lax.dot_general(tok[i], cot[...], (((0,), (0,)), ((), ())), preferred_element_type=f32)

    def pass_on(src, o, to):
        slot = at_z(NZ - src)
        return send(pw.at[:, slot], pw.at[:, slot], pw_s.at[o - 1], pw_r.at[o - 1], zp(to))

    def combine(j):
        xb, o = blocks[j], offs[j]
        core[j].wait_recv()
        total = own[j] + take[j].astype(f32)
        gate = total[:, :, :, :FF].astype(bf16)
        up = total[:, :, :, FF:].astype(bf16)
        for k in range(NY):
            sa[j, k] = gate[:, k]
            sb[k, xb] = up[:, k]
        for k in (2, 1, 3, 0):
            yk = at_y(k)
            if o:
                send(sa.at[j, yk], ra1.at[o - 1, k], a1_s.at[o - 1, k], a1_r.at[o - 1, k], xp(o))
            if k:
                send(sb.at[yk, xb], rb1.at[k - 1, j], b1_s.at[k - 1, j], b1_r.at[k - 1, j], yp(k))

    core = []
    for j in range(NX):
        give[j] = block_grad(2 * j).astype(bf16).reshape(NZ, NY, ROWS, 2 * FF)
        if j == 0:
            pl.semaphore_wait(barrier, len(plane) + len(FAR_Z))
        core.append(send(give.at[j], take.at[j], core_s.at[j], core_r.at[j], mate))
        own[j] = block_grad(2 * j + 1).reshape(NZ, NY, ROWS, 2 * FF)
        if j == 0:
            for cp in load_pw:
                cp.wait()
            pass_on(0, 4, 4)
            pass_on(0, 1, 1)
            pass_on(0, 7, 7)
        else:
            combine(j - 1)
    combine(NX - 1)
    for cp in load_nxt:
        cp.start()


    def second_b(j):
        total = sb[y, blocks[j]].astype(f32)
        for k in range(1, NY):
            arrived(rb1.at[k - 1, j], b1_r.at[k - 1, j])
            total += rb1[k - 1, j].astype(f32)
        tb[j] = total.astype(bf16)
        o = offs[j]
        if o:
            send(tb.at[j], rb2.at[o - 1], b2_s.at[o - 1], b2_r.at[o - 1], xp(o))

    def second_a(k):
        total = sa[NX - 1, at_y(k)].astype(f32)
        for o in range(1, NX):
            arrived(ra1.at[o - 1, k], a1_r.at[o - 1, k])
            total += ra1[o - 1, k].astype(f32)
        ta[k] = total.astype(bf16)
        if k:
            send(ta.at[k], ra2.at[k - 1], a2_s.at[k - 1], a2_r.at[k - 1], yp(k))

    for j in range(NX - 1):
        second_b(j)
    arrived(pw.at[:, at_z(7)], pw_r.at[0])
    pass_on(1, 2, 1)
    arrived(pw.at[:, at_z(1)], pw_r.at[6])
    pass_on(7, 6, 7)
    for k in (2, 1, 3):
        second_a(k)
    second_b(NX - 1)
    second_a(0)

    arrived(pw.at[:, at_z(6)], pw_r.at[1])
    pass_on(2, 3, 1)
    arrived(pw.at[:, at_z(2)], pw_r.at[5])
    pass_on(6, 5, 7)
    total = ta[0].astype(f32)
    for k in range(1, NY):
        arrived(ra2.at[k - 1], a2_r.at[k - 1])
        total += ra2[k - 1].astype(f32)
    tz[:, :, :FF] = total.astype(bf16)
    total = tb[NX - 1].astype(f32)
    for k in range(1, NX):
        arrived(rb2.at[k - 1], b2_r.at[k - 1])
        total += rb2[k - 1].astype(f32)
    tz[:, :, FF:] = total.astype(bf16)

    for o in FAR_Z:
        send(tz.at[at_z(o)], rz.at[o - 1], z_s.at[o - 1], z_r.at[o - 1], zp(o))
    grad = tz[z].astype(f32)
    for o in (1, 7, 2, 6, 3, 5, 4):
        arrived(rz.at[o - 1], z_r.at[o - 1])
        grad += rz[o - 1].astype(f32)

    def fold(t):
        t = t * t
        t = jnp.sum(t, axis=0, keepdims=True)
        return t[:, 0:128] + t[:, 128:256] + t[:, 256:384] + t[:, 384:512]

    sqz[...] = jnp.concatenate([fold(grad[:, :FF]), fold(grad[:, FF:])], axis=0)
    for o in FAR_Z:
        send(sqz, rsqz.at[o - 1], qz_s.at[o - 1], qz_r.at[o - 1], zp(o))
    gz[z] = grad.astype(bf16)
    both = sqz[...]
    for o in (1, 7, 2, 6, 3, 5, 4):
        arrived(rsqz.at[o - 1], qz_r.at[o - 1])
        both += rsqz[o - 1]
    rsq[0] = both
    slots = {o: (o[0] * NC + o[1]) * NY + o[2] for o in plane}
    for o in plane:
        k = slots[o]
        send(rsq.at[0], rsq.at[k], q_s.at[k], q_r.at[k], in_plane(*o))
    for o in FAR_Z:
        send(gz.at[z], gz.at[z], g_s.at[o - 1], g_r.at[o - 1], zp(o))
    for o in (1, 7, 2, 6, 3, 5, 4):
        arrived(gz.at[at_z(NZ - o)], g_r.at[o - 1])
    for o in (3, 5, 4):
        arrived(pw.at[:, at_z(NZ - o)], pw_r.at[o - 1])
    for o in plane[::-1]:
        arrived(rsq.at[slots[o]], q_r.at[slots[o]])
    both = jnp.sum(rsq[...], axis=0)
    limit = math.sqrt(D * FF)
    factor = jnp.minimum(1.0, limit / jnp.sqrt(jnp.sum(both, axis=1, keepdims=True) + 1e-06))
    gate_factor, up_factor = factor[0:1], factor[1:2]
    first_scale = 0.003 / (1.0 - 0.9**10)
    second_scale = 1.0 / (1.0 - 0.95**10)

    def moments(g, slot):
        clipped = jnp.concatenate([g[:, :FF] * gate_factor, g[:, FF:] * up_factor], axis=1)
        return 0.9 * pw[1, slot] + 0.1 * clipped, 0.95 * pw[2, slot] + 0.05 * clipped * clipped

    for k in range(NZ):
        first, second = moments(gz[k].astype(f32), k)
        low = pw[0, k] * (1.0 - 0.003 * 0.1) - (first * first_scale) / (jnp.sqrt(second * second_scale) + 1e-08)
        low = low.astype(bf16)
        wa[x, c, k, y] = low[:, :FF]
        wb[x, c, k, y] = low[:, FF:]

    def pa(ox, oy, lo=0, n=NZ):
        return wa.at[at_x(NX - ox), c, pl.ds(lo, n), at_y(NY - oy)]

    def pb(ox, oy, lo=0, n=NZ):
        return wb.at[at_x(NX - ox), c, pl.ds(lo, n), at_y(NY - oy)]

    def to_mate(piece, ox, oy, ss, rs):
        send(piece(ox, oy), piece(ox, oy), ss.at[ox, oy], rs.at[ox, oy], mate)

    def spread_a(oy):
        for o in (1, 3):
            send(pa(0, oy), pa(0, oy), ga_s.at[o, oy], ga_r.at[o, oy], xp(o))
        to_mate(pa, 0, oy, ca_s, ca_r)

    def spread_b(ox):
        for o in (1, 3):
            send(pb(ox, 0), pb(ox, 0), gb_s.at[ox, o], gb_r.at[ox, o], yp(o))
        to_mate(pb, ox, 0, cb_s, cb_r)

    for o in (1, 3, 2):
        send(pa(0, 0), pa(0, 0), ga_s.at[0, o], ga_r.at[0, o], yp(o))
        send(pb(0, 0), pb(0, 0), gb_s.at[o, 0], gb_r.at[o, 0], xp(o))
    spread_a(0)
    spread_b(0)

    first, second = moments(grad, z)
    nfv[0] = first
    nfv[1] = second
    stores = [pltpu.make_async_copy(nfv.at[i], h, st.at[i]) for i, h in enumerate((nf_hbm, nv_hbm))]
    for cp in stores:
        cp.start()

    half = NZ // 2

    def forward(o):
        arrived(pa(0, o), ga_r.at[0, o])
        spread_a(o)
        arrived(pb(o, 0), gb_r.at[o, 0])
        spread_b(o)

    def relay(k):
        for i, o in enumerate((1, 3)):
            arrived(pa(o, k), ga_r.at[o, k])
            part = pa(o, k, i * half, half)
            send(part, part, ha_s.at[i, k], ha_r.at[i, k], xp(o))
            to_mate(pa, o, k, ca_s, ca_r)
            arrived(pb(k, o), gb_r.at[k, o])
            part = pb(k, o, i * half, half)
            send(part, part, hb_s.at[i, k], hb_r.at[i, k], yp(o))
            to_mate(pb, k, o, cb_s, cb_r)

    def last(k):
        for i in range(2):
            arrived(pa(2, k, i * half, half), ha_r.at[i, k])
            arrived(pb(k, 2, i * half, half), hb_r.at[i, k])
        to_mate(pa, 2, k, ca_s, ca_r)
        to_mate(pb, k, 2, cb_s, cb_r)

    wa_k, wb_k = wa.reshape(NX, 512, FF), wb.reshape(NX, 512, FF)
    theirs_a = wa.at[:, other]
    theirs_b = wb.at[:, other]

    def mate_a(ox):
        for oy in range(NY):
            arrived(theirs_a.at[at_x(NX - ox), :, at_y(NY - oy)], ca_r.at[ox, oy])

    def mate_b(ox):
        for oy in range(NY):
            arrived(theirs_b.at[at_x(NX - ox), :, at_y(NY - oy)], cb_r.at[ox, oy])

    def start_of(acc, w_k):
        k = x

        def tile(i, _):
            r = pl.ds(pl.multiple_of(i * 256, 256), 256)
            acc[r, :] = jnp.dot(nxt[k, r, :], w_k[k], preferred_element_type=f32)
            return 0

        lax.fori_loop(0, TOK // 256, tile, 0)

    def rest():
        ks = [at_x(NX - ox) for ox in (1, 3, 2)]

        def store(i):
            r = pl.ds(pl.multiple_of(i * 256, 256), 256)
            return pltpu.make_async_copy(out.at[r], out_hbm.at[r], st.at[2 + i])

        def tile(i, _):
            r = pl.ds(pl.multiple_of(i * 256, 256), 256)
            gate, up = gate_acc[r, :], up_acc[r, :]
            for k in ks:
                gate += jnp.dot(nxt[k, r, :], wa_k[k], preferred_element_type=f32)
            for k in ks:
                up += jnp.dot(nxt[k, r, :], wb_k[k], preferred_element_type=f32)
            out[r, :] = (gate / (1.0 + jnp.exp(-gate)) * up).astype(bf16)
            store(i).start()
            return 0

        lax.fori_loop(0, TOK // 256, tile, 0)
        stores.extend(store(i) for i in range(TOK // 256))

    forward(1)
    forward(3)
    relay(0)
    forward(2)
    for cp in load_nxt:
        cp.wait()
    relay(1)
    relay(3)
    mate_a(0)
    start_of(gate_acc, wa_k)
    last(0)
    relay(2)
    mate_b(0)
    start_of(up_acc, wb_k)
    last(1)
    last(3)
    last(2)
    for ox in (1, 3, 2):
        mate_a(ox)
        mate_b(ox)
    rest()
    for cp in sent:
        cp.wait_send()
    for cp in stores:
        cp.wait()


def keep(a_ref, b_ref, c_ref, a_out, b_out, c_out, a_buf, b_buf, c_buf, in_sem, out_sem):
    part = TOK // 4
    moves = [(c_ref.at[pl.ds(i * part, part)], c_buf.at[i], c_out.at[pl.ds(i * part, part)]) for i in range(4)]
    moves += [(a_ref, a_buf, a_out), (b_ref, b_buf, b_out)]
    reads = [pltpu.make_async_copy(s, t, in_sem.at[i]) for i, (s, t, _) in enumerate(moves)]
    writes = [pltpu.make_async_copy(t, d, out_sem.at[i]) for i, (_, t, d) in enumerate(moves)]
    for cp in reads:
        cp.start()
    for r, w in zip(reads, writes):
        r.wait()
        w.start()
    for cp in writes:
        cp.wait()


def shards(tokens, grad_out, master_weight, first_moment, second_moment, next_tokens):
    any_ = pl.BlockSpec(memory_space=pltpu.HBM)
    V = pltpu.VMEM
    dma = pltpu.SemaphoreType.DMA

    def pair(*shape):
        return [dma(shape), dma(shape)]

    block = (NX, NZ, NY, ROWS, 2 * FF)
    scratch = [
        V((2 * NX, TOK, 256), bf16), V((TOK, 2 * FF), bf16), V((NX, TOK, 512), bf16), V((3, NZ, ROWS, 2 * FF), f32),
        V(block, f32), V(block, bf16), V(block, bf16),
        V((NX, NY, NZ, ROWS, FF), bf16), V((NY, NX, NZ, ROWS, FF), bf16),
        V((NX - 1, NY, NZ, ROWS, FF), bf16), V((NY - 1, NX, NZ, ROWS, FF), bf16),
        V((NY, NZ, ROWS, FF), bf16), V((NX, NZ, ROWS, FF), bf16),
        V((NY - 1, NZ, ROWS, FF), bf16), V((NX - 1, NZ, ROWS, FF), bf16),
        V((NZ, ROWS, 2 * FF), bf16), V((NZ - 1, ROWS, 2 * FF), bf16),
        V((2, 128), f32), V((NZ - 1, 2, 128), f32), V((NX * NC * NY, 2, 128), f32),
        V((NZ, ROWS, 2 * FF), bf16),
        V((NX, NC, NZ, NY, ROWS, FF), bf16), V((NX, NC, NZ, NY, ROWS, FF), bf16),
        V((TOK, FF), f32), V((TOK, FF), f32), V((2, ROWS, 2 * FF), f32), V((TOK, FF), bf16),
        dma((2 * NX,)), dma((NX,)), dma((4,)),
        *pair(NX), *pair(NX - 1, NY), *pair(NY - 1, NX), *pair(NY - 1), *pair(NX - 1), *pair(NZ - 1),
        *pair(NZ - 1), *pair(NZ - 1), *pair(NX * NC * NY), *pair(NZ - 1),
        *pair(NX, NY), *pair(NX, NY), *pair(2, NY), *pair(2, NX), *pair(NX, NY), *pair(NX, NY), dma((6,)),
    ]
    shapes = (
        jax.ShapeDtypeStruct((ROWS, 2 * FF), f32),
        jax.ShapeDtypeStruct((ROWS, 2 * FF), f32),
        jax.ShapeDtypeStruct((TOK, FF), bf16),
    )
    results = pl.pallas_call(
        body,
        out_shape=shapes,
        in_specs=[any_] * 6,
        out_specs=(any_,) * 3,
        scratch_shapes=scratch,
        compiler_params=pltpu.CompilerParams(
            collective_id=0, has_side_effects=True, vmem_limit_bytes=60 * 1024 * 1024
        ),
    )(tokens, grad_out, master_weight, first_moment, second_moment, next_tokens)
    return pl.pallas_call(
        keep,
        out_shape=shapes,
        in_specs=[any_] * 3,
        out_specs=(any_,) * 3,
        scratch_shapes=[
            V((ROWS, 2 * FF), f32), V((ROWS, 2 * FF), f32), V((4, TOK // 4, FF), bf16), *pair(6),
        ],
        compiler_params=pltpu.CompilerParams(vmem_limit_bytes=60 * 1024 * 1024),
    )(*results)


def solution(mesh):
    split = Mesh(mesh.devices.reshape(NX, NC, NZ, NY), AXES)
    rows = P(AXES, None)
    return jax.shard_map(
        shards, mesh=split, in_specs=(rows,) * 6, out_specs=(rows,) * 3, check_vma=False
    )
```

time: 246 us -> 73.4 us (0.30)
  waiting for transfers between devices: 101 us -> 0 us
  Pallas kernels: 0 us -> 72.6 us
  blocking collectives: 53.4 us -> 0 us
  starting transfers between devices: 28.5 us -> 0 us
  other arithmetic: 19.5 us -> 0 us
  matrix products: 17.4 us -> 0 us
  between operations: 15.7 us -> 0.64 us
  local copies, waits for them, and re-layouts: 9.55 us -> 0 us
    pallas_call x0 -> x2, Pallas kernels: none -> 72.6 us  [the longest x1 70.6 us: shards(): pl.pallas_call(body, out_shape=shapes, in_specs=[any_] * 6, out_specs=(an...]
    all_to_all x4 -> x0, waiting for transfers between devices: 65.9 us -> none  [in_one_piece(): lax.all_to_all(both, axis, split_axis=split_dim, concat_axis=concat_dim,...]
    psum x4 -> x0, blocking collectives: 35.7 us -> none  [one_axis_at_a_time(): return functools.reduce(lax.psum, axes, value)]
    all_gather x1 -> x0, waiting for transfers between devices: 35.4 us -> none  [shards(): whole_weight = lax.all_gather(block_rows, AA, axis=0, tiled=True)]
    all_to_all x4 -> x0, starting transfers between devices: 28.5 us -> none  [in_one_piece(): lax.all_to_all(both, axis, split_axis=split_dim, concat_axis=concat_dim,...]
    all_to_all x1 -> x0, blocking collectives: 17.7 us -> none  [from_everyone(): return lax.all_to_all(copies, axis, split_axis=0, concat_axis=0, tiled=True)]
    dot_general x3 -> x0, matrix products: 17.4 us -> none  [the longest x2 9.83 us: reduce_tensor(): lax.dot_general(tokens, cotangent, (((0,), (0,)), ((), ())), preferred_el...]
    convert_element_type x12 -> x0, other arithmetic: 7.17 us -> none  [the longest x4 5.83 us: encode_blocks(): (blocks / scales.astype(jnp.float32)[:, :, None]).astype(jnp.bfloat16)]
  transfers between devices with their start and end apart: 5 -> 0, of which waited for: 5 -> 0; matrix products, arithmetic and copies ran while one was open for 7% -> 0% of each run, Pallas kernels for 0% -> 0%
where the time goes in v2:
time: 73.4 us; the launch traced here: 73.3 us
  Pallas kernels  72.6 us (99%)
    pallas_call x1, Pallas kernels, shards(): pl.pallas_call(body, out_shape=shapes, in_specs=[any_] * 6, out_specs=(an...  70.6 us
    pallas_call x1, Pallas kernels, shards(): pl.pallas_call(keep, out_shape=shapes, in_specs=[any_] * 3, out_specs=(an...  2.03 us

profile of v2, /device:TPU:1, one launch (start us, length us, event | category | flops | bytes accessed | tf_op | source)
XLA Modules:
  0.0 73.3 jit_solution(7907474646658416554)
XLA Ops:
  0.6 70.6 %shard_map.85 = (f32[8,1024]{1,0:T(8,128)}, f32[8,1024]{1,0:T(8,128)}, bf16[1024,512]{1,0:T(8,128)(2,1)}) custom-call(bf16[1024,2048]{1,0:T(8,128)(2,1)} %tok_hbm.1, bf16[1024,1024]{1,0:T(8,128)(2,1)} %cot_hbm.1, f32[8,1024]{1,0:T(8,128)} %w_hbm.1, f32[8,1024]{1,0:T(8,128)} %m_hbm.1, f32[8,1024]{1,0:T(8,128)} %v_hbm.1, bf16[1024,2048]{1,0:T(8,128)(2,1)} %nxt_hbm.1), custom_call_target="tpu_custom_call" | custom-call | tf_op jit(solution)/shard_map/pallas_call | solution.py:421
  71.2 2.0 %shard_map.86 = (f32[8,1024]{1,0:T(8,128)}, f32[8,1024]{1,0:T(8,128)}, bf16[1024,512]{1,0:T(8,128)(2,1)}) custom-call(f32[8,1024]{1,0:T(8,128)} %get-tuple-element.6.a_ref, f32[8,1024]{1,0:T(8,128)} %get-tuple-element.7.b_ref, bf16[1024,512]{1,0:T(8,128)(2,1)} %get-tuple-element.8.c_ref), custom_call_target="tpu_custom_call" | custom-call | tf_op jit(solution)/shard_map/pallas_call | solution.py:431

commit v3 on v2

v3 whole, which is shorter than its diff:
```python
import math

import jax
import jax.numpy as jnp
from jax import lax
from jax.experimental import pallas as pl
from jax.experimental.pallas import tpu as pltpu
from jax.sharding import Mesh
from jax.sharding import PartitionSpec as P

NX, NC, NZ, NY = 4, 2, 8, 4
ROWS = 8
D = 2048
FF = 512
TOK = 1024
AXES = ("x", "c", "z", "y")
MESH = pl.DeviceIdType.MESH
FAR_Z = (4, 3, 5, 2, 6, 1, 7)
f32 = jnp.float32
bf16 = jnp.bfloat16


def body(
    tok_hbm, cot_hbm, w_hbm, m_hbm, v_hbm, nxt_hbm,
    nf_hbm, nv_hbm, out_hbm,
    tok, cot, nxt, pw, own, give, take,
    sa, sb, fa, fb, ra1, rb1, ta, tb, ra2, rb2, tz, rz, sqz, rsqz, rsq, gz, wa, wb, gate_acc, up_acc, nfv, out,
    ld_t, ld_n, ld, st, done, core_r, fa_r, fb_r, a1_r, b1_r, a2_r, b2_r, z_r, pw_r, qz_r, q_r, g_r,
    ga_r, gb_r, na_r, nb_r, ha_r, hb_r, ca_r, cb_r,
):
    x, c, z, y = (lax.axis_index(a) for a in AXES)
    other = 1 - c

    def at_x(o):
        return lax.rem(x + o, NX)

    def at_y(o):
        return lax.rem(y + o, NY)

    def at_z(o):
        return lax.rem(z + o, NZ)

    def xp(o):
        return {"x": at_x(o)}

    def yp(o):
        return {"y": at_y(o)}

    def zp(o):
        return {"z": at_z(o)}

    mate = {"c": other}
    plane = [
        (ox, oc, oy) for ox in (2, 1, 3, 0) for oy in (2, 1, 3, 0) for oc in (1, 0) if ox or oc or oy
    ]

    def in_plane(ox, oc, oy):
        return {"x": at_x(ox), "c": other if oc else c, "y": at_y(oy)}

    CORE, A1, B1, A2, B2, Z, PW, QZ, Q, G, GA, GB, CA, CB = range(14)

    def send(src, dst, kind, rs, to):
        pltpu.make_async_remote_copy(
            src_ref=src, dst_ref=dst, send_sem=done.at[kind], recv_sem=rs, device_id=to, device_id_type=MESH
        ).start()

    def handle(ref, sem):
        return pltpu.make_async_remote_copy(
            src_ref=ref, dst_ref=ref, send_sem=sem, recv_sem=sem, device_id=mate, device_id_type=MESH
        )

    def arrived(dst, rs):
        handle(dst, rs).wait_recv()

    barrier = pltpu.get_barrier_semaphore()
    for o in plane:
        pl.semaphore_signal(barrier, inc=1, device_id=in_plane(*o), device_id_type=MESH)
    for o in FAR_Z:
        pl.semaphore_signal(barrier, inc=1, device_id=zp(o), device_id_type=MESH)

    offs = (2, 1, 3, 0)
    blocks = [at_x(o) for o in offs]
    load_cot = pltpu.make_async_copy(cot_hbm, cot, ld.at[0])
    load_tok = []
    for j in range(NX):
        for i, cc in enumerate((other, c)):
            start = pl.multiple_of(blocks[j] * 512 + cc * 256, 256)
            load_tok.append(
                pltpu.make_async_copy(tok_hbm.at[:, pl.ds(start, 256)], tok.at[2 * j + i], ld_t.at[2 * j + i])
            )
    load_pw = [
        pltpu.make_async_copy(h, pw.at[i, z], ld.at[1 + i]) for i, h in enumerate((w_hbm, m_hbm, v_hbm))
    ]
    load_nxt = [
        pltpu.make_async_copy(nxt_hbm.at[:, pl.ds(k * 512, 512)], nxt.at[k], ld_n.at[k]) for k in range(NX)
    ]
    for cp in [load_tok[0], load_cot, load_tok[1]]:
        cp.start()
    load_cot.wait()
    load_tok[0].wait()
    for cp in load_tok[2:] + load_pw:
        cp.start()

    def block_grad(i):
        if i:
            load_tok[i].wait()
        return lax.dot_general(tok[i], cot[...], (((0,), (0,)), ((), ())), preferred_element_type=f32)

    def pass_on(src, o, to):
        slot = at_z(NZ - src)
        send(pw.at[:, slot], pw.at[:, slot], PW, pw_r.at[o - 1], zp(to))

    half = NZ // 2
    lower, upper = pl.ds(0, half), pl.ds(half, half)
    whole = pl.ds(0, NZ)
    via_next, via_prev = (2, 0), (1, 3)

    def gate_sum(j, k, zs=whole):
        yk = at_y(k)
        return own[j, zs, yk, :, pl.ds(0, FF)] + take[j, zs, yk, :, pl.ds(0, FF)].astype(f32)

    def up_sum(j, k, zs=whole):
        yk = at_y(k)
        return own[j, zs, yk, :, pl.ds(FF, FF)] + take[j, zs, yk, :, pl.ds(FF, FF)].astype(f32)

    def near_a(j, k, value):
        sa[j, k] = value.astype(bf16)
        send(sa.at[j, k], ra1.at[k, j - 1], A1, a1_r.at[k], xp(1 if j == 1 else 3))

    def near_b(j, i, zs, value):
        sb[j, 1 + i, zs] = value.astype(bf16)
        send(sb.at[j, 1 + i, zs], rb1.at[j, i, zs], B1, b1_r.at[j], yp((1, 3)[i]))

    def combine(j):
        arrived(take.at[j], core_r.at[j])
        if j == 0:
            for k in (2, 1, 0, 3):
                sa[0, k] = gate_sum(0, k).astype(bf16)
                i, n = (0, via_next.index(k)) if k in via_next else (1, via_prev.index(k))
                send(sa.at[0, k], fa.at[i, n], A1, fa_r.at[i], xp(1 if i == 0 else 3))
        sb[j, 0] = up_sum(j, 2).astype(bf16)
        for zs, o in ((lower, 1), (upper, 3)):
            send(sb.at[j, 0, zs], fb.at[j, zs], B1, fb_r.at[j], yp(o))
        near_b(j, 0, upper, up_sum(j, 1, upper))
        near_b(j, 1, lower, up_sum(j, 3, lower))
        if j == 1:
            for k in via_prev:
                near_a(1, k, gate_sum(1, k))
        if j == 2:
            for k in via_next:
                near_a(2, k, gate_sum(2, k))

    def add_a(i):
        arrived(fa.at[i], fa_r.at[i])
        for n, k in enumerate((via_next, via_prev)[i]):
            near_a(1 + i, k, gate_sum(1 + i, k) + fa[i, n].astype(f32))

    def add_b(j):
        arrived(fb.at[j], fb_r.at[j])
        near_b(j, 0, lower, up_sum(j, 1, lower) + fb[j, lower].astype(f32))
        near_b(j, 1, upper, up_sum(j, 3, upper) + fb[j, upper].astype(f32))

    def second_a(k):
        total = gate_sum(NX - 1, k)
        arrived(ra1.at[k], a1_r.at[k])
        total += ra1[k, 0].astype(f32) + ra1[k, 1].astype(f32)
        if k:
            ta[k - 1] = total.astype(bf16)
            send(ta.at[k - 1], ra2.at[k - 1], A2, a2_r.at[0], yp(k))
        return total

    def second_b(j):
        total = up_sum(j, 0)
        arrived(rb1.at[j], b1_r.at[j])
        total += rb1[j, 0].astype(f32) + rb1[j, 1].astype(f32)
        o = offs[j]
        if o:
            tb[o - 1] = total.astype(bf16)
            send(tb.at[o - 1], rb2.at[o - 1], B2, b2_r.at[0], xp(o))
        return total

    for j in range(NX):
        give[j] = block_grad(2 * j).astype(bf16).reshape(NZ, NY, ROWS, 2 * FF)
        if j == 0:
            pl.semaphore_wait(barrier, len(plane) + len(FAR_Z))
        send(give.at[j], take.at[j], CORE, core_r.at[j], mate)
        own[j] = block_grad(2 * j + 1).reshape(NZ, NY, ROWS, 2 * FF)
        if j == 0:
            for cp in load_pw:
                cp.wait()
            pass_on(0, 4, 4)
            pass_on(0, 1, 1)
            pass_on(0, 7, 7)
        else:
            combine(j - 1)
    combine(NX - 1)
    for cp in load_nxt:
        cp.start()
    add_a(0)
    add_b(0)
    add_a(1)
    add_b(1)
    add_b(2)
    add_b(3)
    second_b(0)
    arrived(pw.at[:, at_z(7)], pw_r.at[0])
    pass_on(1, 2, 1)
    arrived(pw.at[:, at_z(1)], pw_r.at[6])
    pass_on(7, 6, 7)
    second_a(2)
    second_a(1)
    second_b(1)
    second_b(2)
    second_a(3)
    total = second_a(0)
    arrived(ra2, a2_r.at[0])
    for k in range(NY - 1):
        total += ra2[k].astype(f32)
    tz[:, :, :FF] = total.astype(bf16)
    total = second_b(NX - 1)
    arrived(rb2, b2_r.at[0])
    for k in range(NX - 1):
        total += rb2[k].astype(f32)
    tz[:, :, FF:] = total.astype(bf16)

    for o in FAR_Z:
        send(tz.at[at_z(o)], rz.at[o - 1], Z, z_r.at[0], zp(o))
    arrived(pw.at[:, at_z(6)], pw_r.at[1])
    pass_on(2, 3, 1)
    arrived(pw.at[:, at_z(2)], pw_r.at[5])
    pass_on(6, 5, 7)
    grad = tz[z].astype(f32)
    arrived(rz, z_r.at[0])
    for o in range(NZ - 1):
        grad += rz[o].astype(f32)

    def fold(t):
        t = t * t
        t = jnp.sum(t, axis=0, keepdims=True)
        return t[:, 0:128] + t[:, 128:256] + t[:, 256:384] + t[:, 384:512]

    sqz[...] = jnp.concatenate([fold(grad[:, :FF]), fold(grad[:, FF:])], axis=0)
    for o in FAR_Z:
        send(sqz, rsqz.at[o - 1], QZ, qz_r.at[0], zp(o))
    gz[0] = grad.astype(bf16)
    both = sqz[...]
    arrived(rsqz, qz_r.at[0])
    for o in range(NZ - 1):
        both += rsqz[o]
    rsq[0] = both
    for i, o in enumerate(plane):
        send(rsq.at[0], rsq.at[1 + i], Q, q_r.at[0], in_plane(*o))
    for o in FAR_Z:
        send(gz.at[0], gz.at[o], G, g_r.at[0], zp(o))
    arrived(gz.at[pl.ds(1, NZ - 1)], g_r.at[0])
    for o in (3, 5, 4):
        arrived(pw.at[:, at_z(NZ - o)], pw_r.at[o - 1])
    arrived(rsq.at[pl.ds(1, len(plane))], q_r.at[0])
    both = jnp.sum(rsq[...], axis=0)
    limit = math.sqrt(D * FF)
    factor = jnp.minimum(1.0, limit / jnp.sqrt(jnp.sum(both, axis=1, keepdims=True) + 1e-06))
    gate_factor, up_factor = factor[0:1], factor[1:2]
    first_scale = 0.003 / (1.0 - 0.9**10)
    second_scale = 1.0 / (1.0 - 0.95**10)

    def moments(g, slot):
        clipped = jnp.concatenate([g[:, :FF] * gate_factor, g[:, FF:] * up_factor], axis=1)
        return 0.9 * pw[1, slot] + 0.1 * clipped, 0.95 * pw[2, slot] + 0.05 * clipped * clipped

    for o in range(NZ):
        k = at_z(NZ - o)
        first, second = moments(gz[o].astype(f32), k)
        low = pw[0, k] * (1.0 - 0.003 * 0.1) - (first * first_scale) / (jnp.sqrt(second * second_scale) + 1e-08)
        low = low.astype(bf16)
        wa[x, c, k, y] = low[:, :FF]
        wb[x, c, k, y] = low[:, FF:]

    def pa(ox, oy, lo=0, n=NZ):
        return wa.at[at_x(NX - ox), c, pl.ds(lo, n), at_y(NY - oy)]

    def pb(ox, oy, lo=0, n=NZ):
        return wb.at[at_x(NX - ox), c, pl.ds(lo, n), at_y(NY - oy)]

    def to_mate_a(ox, oy):
        send(pa(ox, oy), pa(ox, oy), CA, ca_r.at[ox], mate)

    def to_mate_b(ox, oy):
        send(pb(ox, oy), pb(ox, oy), CB, cb_r.at[ox], mate)

    def spread_a(oy):
        for i, o in enumerate((1, 3)):
            send(pa(0, oy), pa(0, oy), GA, na_r.at[i, oy], xp(o))
        to_mate_a(0, oy)

    def spread_b(ox):
        for i, o in enumerate((1, 3)):
            send(pb(ox, 0), pb(ox, 0), GB, nb_r.at[i, ox], yp(o))
        to_mate_b(ox, 0)

    for o in (1, 3, 2):
        send(pa(0, 0), pa(0, 0), GA, ga_r.at[o - 1], yp(o))
        send(pb(0, 0), pb(0, 0), GB, gb_r.at[o - 1], xp(o))
    spread_a(0)
    spread_b(0)

    first, second = moments(grad, z)
    nfv[0] = first
    nfv[1] = second
    stores = [pltpu.make_async_copy(nfv.at[i], h, st.at[i]) for i, h in enumerate((nf_hbm, nv_hbm))]
    for cp in stores:
        cp.start()

    def forward(o):
        arrived(pa(0, o), ga_r.at[o - 1])
        spread_a(o)
        arrived(pb(o, 0), gb_r.at[o - 1])
        spread_b(o)

    def relay(k):
        for i, o in enumerate((1, 3)):
            arrived(pa(o, k), na_r.at[i, k])
            part = pa(o, k, i * half, half)
            send(part, part, GA, ha_r.at[k], xp(o))
            to_mate_a(o, k)
            arrived(pb(k, o), nb_r.at[i, k])
            part = pb(k, o, i * half, half)
            send(part, part, GB, hb_r.at[k], yp(o))
            to_mate_b(k, o)

    def last(k):
        arrived(pa(2, k), ha_r.at[k])
        to_mate_a(2, k)
        arrived(pb(k, 2), hb_r.at[k])
        to_mate_b(k, 2)

    wa_k, wb_k = wa.reshape(NX, 512, FF), wb.reshape(NX, 512, FF)
    def mate_a(ox):
        arrived(wa.at[at_x(NX - ox), other], ca_r.at[ox])

    def mate_b(ox):
        arrived(wb.at[at_x(NX - ox), other], cb_r.at[ox])

    def start_of(acc, w_k):
        k = x

        def tile(i, _):
            r = pl.ds(pl.multiple_of(i * 256, 256), 256)
            acc[r, :] = jnp.dot(nxt[k, r, :], w_k[k], preferred_element_type=f32)
            return 0

        lax.fori_loop(0, TOK // 256, tile, 0)

    def rest():
        ks = [at_x(NX - ox) for ox in (1, 3, 2)]

        def store(i):
            r = pl.ds(pl.multiple_of(i * 256, 256), 256)
            return pltpu.make_async_copy(out.at[r], out_hbm.at[r], st.at[2 + i])

        def tile(i, _):
            r = pl.ds(pl.multiple_of(i * 256, 256), 256)
            gate, up = gate_acc[r, :], up_acc[r, :]
            for k in ks:
                gate += jnp.dot(nxt[k, r, :], wa_k[k], preferred_element_type=f32)
            for k in ks:
                up += jnp.dot(nxt[k, r, :], wb_k[k], preferred_element_type=f32)
            out[r, :] = (gate / (1.0 + jnp.exp(-gate)) * up).astype(bf16)
            store(i).start()
            return 0

        lax.fori_loop(0, TOK // 256, tile, 0)
        stores.extend(store(i) for i in range(TOK // 256))

    forward(1)
    forward(3)
    relay(0)
    forward(2)
    for cp in load_nxt:
        cp.wait()
    relay(1)
    relay(3)
    relay(2)
    last(0)
    mate_a(0)
    start_of(gate_acc, wa_k)
    last(1)
    last(3)
    mate_b(0)
    start_of(up_acc, wb_k)
    last(2)
    for ox in (1, 3, 2):
        mate_a(ox)
        mate_b(ox)
    rest()
    rows64 = pl.ds(0, 15 * 64)
    bytes_of = {
        CORE: give, A1: sa, B1: sb, A2: ta, B2: tb, Z: tz.at[pl.ds(0, NZ - 1)], PW: pw.at[:, pl.ds(0, NZ - 1)],
        QZ: rsqz, Q: rsq.at[pl.ds(1, len(plane))], G: gz.at[pl.ds(1, NZ - 1)],
        GA: wa.reshape(D, FF).at[rows64], GB: wb.reshape(D, FF).at[rows64], CA: wa.at[:, c], CB: wb.at[:, c],
    }
    for kind, ref in bytes_of.items():
        handle(ref, done.at[kind]).wait_send()
    for cp in stores:
        cp.wait()


def keep(a_ref, b_ref, c_ref, a_out, b_out, c_out, a_buf, b_buf, c_buf, in_sem, out_sem):
    part = TOK // 4
    moves = [(c_ref.at[pl.ds(i * part, part)], c_buf.at[i], c_out.at[pl.ds(i * part, part)]) for i in range(4)]
    moves += [(a_ref, a_buf, a_out), (b_ref, b_buf, b_out)]
    reads = [pltpu.make_async_copy(s, t, in_sem.at[i]) for i, (s, t, _) in enumerate(moves)]
    writes = [pltpu.make_async_copy(t, d, out_sem.at[i]) for i, (_, t, d) in enumerate(moves)]
    for cp in reads:
        cp.start()
    for r, w in zip(reads, writes):
        r.wait()
        w.start()
    for cp in writes:
        cp.wait()


def shards(tokens, grad_out, master_weight, first_moment, second_moment, next_tokens):
    any_ = pl.BlockSpec(memory_space=pltpu.HBM)
    V = pltpu.VMEM
    dma = pltpu.SemaphoreType.DMA

    block = (NX, NZ, NY, ROWS, 2 * FF)
    piece = (NZ, ROWS, FF)
    scratch = [
        V((2 * NX, TOK, 256), bf16), V((TOK, 2 * FF), bf16), V((NX, TOK, 512), bf16), V((3, NZ, ROWS, 2 * FF), f32),
        V(block, f32), V(block, bf16), V(block, bf16),
        V((NX - 1, NY, *piece), bf16), V((NX, NY - 1, *piece), bf16), V((2, 2, *piece), bf16), V((NX, *piece), bf16),
        V((NY, 2, *piece), bf16), V((NX, 2, *piece), bf16),
        V((NY - 1, *piece), bf16), V((NX - 1, *piece), bf16), V((NY - 1, *piece), bf16), V((NX - 1, *piece), bf16),
        V((NZ, ROWS, 2 * FF), bf16), V((NZ - 1, ROWS, 2 * FF), bf16),
        V((2, 128), f32), V((NZ - 1, 2, 128), f32), V((NX * NC * NY, 2, 128), f32),
        V((NZ, ROWS, 2 * FF), bf16),
        V((NX, NC, NZ, NY, ROWS, FF), bf16), V((NX, NC, NZ, NY, ROWS, FF), bf16),
        V((TOK, FF), f32), V((TOK, FF), f32), V((2, ROWS, 2 * FF), f32), V((TOK, FF), bf16),
        dma((2 * NX,)), dma((NX,)), dma((4,)), dma((6,)), dma((14,)),
        dma((NX,)), dma((2,)), dma((NX,)), dma((NY,)), dma((NX,)), dma((1,)), dma((1,)), dma((1,)),
        dma((NZ - 1,)), dma((1,)), dma((1,)), dma((1,)),
        dma((NY - 1,)), dma((NX - 1,)), dma((2, NY)), dma((2, NX)), dma((NY,)), dma((NX,)), dma((NX,)), dma((NX,)),
    ]
    shapes = (
        jax.ShapeDtypeStruct((ROWS, 2 * FF), f32),
        jax.ShapeDtypeStruct((ROWS, 2 * FF), f32),
        jax.ShapeDtypeStruct((TOK, FF), bf16),
    )
    results = pl.pallas_call(
        body,
        out_shape=shapes,
        in_specs=[any_] * 6,
        out_specs=(any_,) * 3,
        scratch_shapes=scratch,
        compiler_params=pltpu.CompilerParams(
            collective_id=0, has_side_effects=True, vmem_limit_bytes=60 * 1024 * 1024
        ),
    )(tokens, grad_out, master_weight, first_moment, second_moment, next_tokens)
    return pl.pallas_call(
        keep,
        out_shape=shapes,
        in_specs=[any_] * 3,
        out_specs=(any_,) * 3,
        scratch_shapes=[
            V((ROWS, 2 * FF), f32), V((ROWS, 2 * FF), f32), V((4, TOK // 4, FF), bf16),
            dma((6,)), dma((6,)),
        ],
        compiler_params=pltpu.CompilerParams(vmem_limit_bytes=60 * 1024 * 1024),
    )(*results)


def solution(mesh):
    split = Mesh(mesh.devices.reshape(NX, NC, NZ, NY), AXES)
    rows = P(AXES, None)
    return jax.shard_map(
        shards, mesh=split, in_specs=(rows,) * 6, out_specs=(rows,) * 3, check_vma=False
    )
```

time: 73.4 us -> 68.6 us (0.935)
  Pallas kernels: 72.6 us -> 67.9 us
    pallas_call x1, Pallas kernels: 70.6 us -> 65.8 us  [shards(): pl.pallas_call(body, out_shape=shapes, in_specs=[any_] * 6, out_specs=(an...]
where the time goes in v3:
time: 68.6 us; the launch traced here: 68.5 us
  Pallas kernels  67.9 us (99%)
    pallas_call x1, Pallas kernels, shards(): pl.pallas_call(body, out_shape=shapes, in_specs=[any_] * 6, out_specs=(an...  65.8 us
    pallas_call x1, Pallas kernels, shards(): pl.pallas_call(keep, out_shape=shapes, in_specs=[any_] * 3, out_specs=(an...  2.03 us

profile of v3, /device:TPU:1, one launch (start us, length us, event | category | flops | bytes accessed | tf_op | source)
XLA Modules:
  0.0 68.5 jit_solution(8429946805877752098)
XLA Ops:
  0.6 65.8 %shard_map.85 = (f32[8,1024]{1,0:T(8,128)}, f32[8,1024]{1,0:T(8,128)}, bf16[1024,512]{1,0:T(8,128)(2,1)}) custom-call(bf16[1024,2048]{1,0:T(8,128)(2,1)} %tok_hbm.1, bf16[1024,1024]{1,0:T(8,128)(2,1)} %cot_hbm.1, f32[8,1024]{1,0:T(8,128)} %w_hbm.1, f32[8,1024]{1,0:T(8,128)} %m_hbm.1, f32[8,1024]{1,0:T(8,128)} %v_hbm.1, bf16[1024,2048]{1,0:T(8,128)(2,1)} %nxt_hbm.1), custom_call_target="tpu_custom_call" | custom-call | tf_op jit(solution)/shard_map/pallas_call | solution.py:450
  66.5 2.0 %shard_map.86 = (f32[8,1024]{1,0:T(8,128)}, f32[8,1024]{1,0:T(8,128)}, bf16[1024,512]{1,0:T(8,128)(2,1)}) custom-call(f32[8,1024]{1,0:T(8,128)} %get-tuple-element.6.a_ref, f32[8,1024]{1,0:T(8,128)} %get-tuple-element.7.b_ref, bf16[1024,512]{1,0:T(8,128)(2,1)} %get-tuple-element.8.c_ref), custom_call_target="tpu_custom_call" | custom-call | tf_op jit(solution)/shard_map/pallas_call | solution.py:460

commit v4 on v3

--- a/solution.py
+++ b/solution.py
@@ -22,10 +22,10 @@
 
 def body(
     tok_hbm, cot_hbm, w_hbm, m_hbm, v_hbm, nxt_hbm,
-    nf_hbm, nv_hbm, out_hbm,
+    nf_ref, nv_ref, out_ref,
     tok, cot, nxt, pw, own, give, take,
-    sa, sb, fa, fb, ra1, rb1, ta, tb, ra2, rb2, tz, rz, sqz, rsqz, rsq, gz, wa, wb, gate_acc, up_acc, nfv, out,
-    ld_t, ld_n, ld, st, done, core_r, fa_r, fb_r, a1_r, b1_r, a2_r, b2_r, z_r, pw_r, qz_r, q_r, g_r,
+    sa, sb, fa, fb, ra1, rb1, ta, tb, ra2, rb2, tz, rz, sqz, rsqz, rsq, gz, wa, wb, gate_acc, up_acc,
+    ld_t, ld, done, core_r, fa_r, fb_r, a1_r, b1_r, a2_r, b2_r, z_r, pw_r, qz_r, q_r, g_r,
     ga_r, gb_r, na_r, nb_r, ha_r, hb_r, ca_r, cb_r,
 ):
     x, c, z, y = (lax.axis_index(a) for a in AXES)
@@ -80,7 +80,9 @@
 
     offs = (2, 1, 3, 0)
     blocks = [at_x(o) for o in offs]
-    load_cot = pltpu.make_async_copy(cot_hbm, cot, ld.at[0])
+    load_cot = [
+        pltpu.make_async_copy(cot_hbm.at[:, pl.ds(i * FF, FF)], cot.at[i], ld.at[3 + i]) for i in range(2)
+    ]
     load_tok = []
     for j in range(NX):
         for i, cc in enumerate((other, c)):
@@ -89,22 +91,19 @@
                 pltpu.make_async_copy(tok_hbm.at[:, pl.ds(start, 256)], tok.at[2 * j + i], ld_t.at[2 * j + i])
             )
     load_pw = [
-        pltpu.make_async_copy(h, pw.at[i, z], ld.at[1 + i]) for i, h in enumerate((w_hbm, m_hbm, v_hbm))
+        pltpu.make_async_copy(h, pw.at[i, z], ld.at[i]) for i, h in enumerate((w_hbm, m_hbm, v_hbm))
     ]
     load_nxt = [
-        pltpu.make_async_copy(nxt_hbm.at[:, pl.ds(k * 512, 512)], nxt.at[k], ld_n.at[k]) for k in range(NX)
+        pltpu.make_async_copy(nxt_hbm.at[:, pl.ds(k * 512, 512)], nxt.at[k], ld.at[5]) for k in range(NX)
     ]
-    for cp in [load_tok[0], load_cot, load_tok[1]]:
+    for cp in [load_cot[0], load_tok[0], load_cot[1], load_tok[1]]:
         cp.start()
-    load_cot.wait()
-    load_tok[0].wait()
-    for cp in load_tok[2:] + load_pw:
-        cp.start()
-
-    def block_grad(i):
-        if i:
-            load_tok[i].wait()
-        return lax.dot_general(tok[i], cot[...], (((0,), (0,)), ((), ())), preferred_element_type=f32)
+
+    def rows_of(i):
+        return jnp.transpose(tok[i])
+
+    def block_grad(lhs, h):
+        return jnp.dot(lhs, cot[h], preferred_element_type=f32).reshape(NZ, NY, ROWS, FF)
 
     def pass_on(src, o, to):
         slot = at_z(NZ - src)
@@ -117,11 +116,11 @@
 
     def gate_sum(j, k, zs=whole):
         yk = at_y(k)
-        return own[j, zs, yk, :, pl.ds(0, FF)] + take[j, zs, yk, :, pl.ds(0, FF)].astype(f32)
+        return own[j, 0, zs, yk] + take[j, 0, zs, yk].astype(f32)
 
     def up_sum(j, k, zs=whole):
         yk = at_y(k)
-        return own[j, zs, yk, :, pl.ds(FF, FF)] + take[j, zs, yk, :, pl.ds(FF, FF)].astype(f32)
+        return own[j, 1, zs, yk] + take[j, 1, zs, yk].astype(f32)
 
     def near_a(j, k, value):
         sa[j, k] = value.astype(bf16)
@@ -131,24 +130,27 @@
         sb[j, 1 + i, zs] = value.astype(bf16)
         send(sb.at[j, 1 + i, zs], rb1.at[j, i, zs], B1, b1_r.at[j], yp((1, 3)[i]))
 
-    def combine(j):
-        arrived(take.at[j], core_r.at[j])
+    def combine_gate(j):
+        arrived(take.at[j, 0], core_r.at[j, 0])
         if j == 0:
             for k in (2, 1, 0, 3):
                 sa[0, k] = gate_sum(0, k).astype(bf16)
                 i, n = (0, via_next.index(k)) if k in via_next else (1, via_prev.index(k))
                 send(sa.at[0, k], fa.at[i, n], A1, fa_r.at[i], xp(1 if i == 0 else 3))
-        sb[j, 0] = up_sum(j, 2).astype(bf16)
-        for zs, o in ((lower, 1), (upper, 3)):
-            send(sb.at[j, 0, zs], fb.at[j, zs], B1, fb_r.at[j], yp(o))
-        near_b(j, 0, upper, up_sum(j, 1, upper))
-        near_b(j, 1, lower, up_sum(j, 3, lower))
         if j == 1:
             for k in via_prev:
                 near_a(1, k, gate_sum(1, k))
         if j == 2:
             for k in via_next:
                 near_a(2, k, gate_sum(2, k))
+
+    def combine_up(j):
+        arrived(take.at[j, 1], core_r.at[j, 1])
+        sb[j, 0] = up_sum(j, 2).astype(bf16)
+        for zs, o in ((lower, 1), (upper, 3)):
+            send(sb.at[j, 0, zs], fb.at[j, zs], B1, fb_r.at[j], yp(o))
+        near_b(j, 0, upper, up_sum(j, 1, upper))
+        near_b(j, 1, lower, up_sum(j, 3, lower))
 
     def add_a(i):
         arrived(fa.at[i], fa_r.at[i])
@@ -179,21 +181,41 @@
             send(tb.at[o - 1], rb2.at[o - 1], B2, b2_r.at[0], xp(o))
         return total
 
+    def give_send(j, h):
+        send(give.at[j, h], take.at[j, h], CORE, core_r.at[j, h], mate)
+
     for j in range(NX):
-        give[j] = block_grad(2 * j).astype(bf16).reshape(NZ, NY, ROWS, 2 * FF)
+        if j:
+            load_tok[2 * j].wait()
+        else:
+            load_cot[0].wait()
+            load_tok[0].wait()
+            for cp in load_tok[2:] + load_pw:
+                cp.start()
+        lhs = rows_of(2 * j)
+        give[j, 0] = block_grad(lhs, 0).astype(bf16)
         if j == 0:
             pl.semaphore_wait(barrier, len(plane) + len(FAR_Z))
-        send(give.at[j], take.at[j], CORE, core_r.at[j], mate)
-        own[j] = block_grad(2 * j + 1).reshape(NZ, NY, ROWS, 2 * FF)
+        give_send(j, 0)
+        if j == 0:
+            load_cot[1].wait()
+        give[j, 1] = block_grad(lhs, 1).astype(bf16)
+        give_send(j, 1)
+        if j:
+            combine_gate(j - 1)
+            combine_up(j - 1)
+        load_tok[2 * j + 1].wait()
+        lhs = rows_of(2 * j + 1)
+        own[j, 0] = block_grad(lhs, 0)
+        own[j, 1] = block_grad(lhs, 1)
         if j == 0:
             for cp in load_pw:
                 cp.wait()
-            pass_on(0, 4, 4)
             pass_on(0, 1, 1)
             pass_on(0, 7, 7)
-        else:
-            combine(j - 1)
-    combine(NX - 1)
+            pass_on(0, 4, 4)
+    combine_gate(NX - 1)
+    combine_up(NX - 1)
     for cp in load_nxt:
         cp.start()
     add_a(0)
@@ -202,17 +224,21 @@
     add_b(1)
     add_b(2)
     add_b(3)
-    second_b(0)
     arrived(pw.at[:, at_z(7)], pw_r.at[0])
     pass_on(1, 2, 1)
     arrived(pw.at[:, at_z(1)], pw_r.at[6])
     pass_on(7, 6, 7)
+    second_b(0)
     second_a(2)
     second_a(1)
     second_b(1)
     second_b(2)
     second_a(3)
     total = second_a(0)
+    arrived(pw.at[:, at_z(6)], pw_r.at[1])
+    pass_on(2, 3, 1)
+    arrived(pw.at[:, at_z(2)], pw_r.at[5])
+    pass_on(6, 5, 7)
     arrived(ra2, a2_r.at[0])
     for k in range(NY - 1):
         total += ra2[k].astype(f32)
@@ -225,10 +251,6 @@
 
     for o in FAR_Z:
         send(tz.at[at_z(o)], rz.at[o - 1], Z, z_r.at[0], zp(o))
-    arrived(pw.at[:, at_z(6)], pw_r.at[1])
-    pass_on(2, 3, 1)
-    arrived(pw.at[:, at_z(2)], pw_r.at[5])
-    pass_on(6, 5, 7)
     grad = tz[z].astype(f32)
     arrived(rz, z_r.at[0])
     for o in range(NZ - 1):
@@ -304,11 +326,8 @@
     spread_b(0)
 
     first, second = moments(grad, z)
-    nfv[0] = first
-    nfv[1] = second
-    stores = [pltpu.make_async_copy(nfv.at[i], h, st.at[i]) for i, h in enumerate((nf_hbm, nv_hbm))]
-    for cp in stores:
-        cp.start()
+    nf_ref[...] = first
+    nv_ref[...] = second
 
     def forward(o):
         arrived(pa(0, o), ga_r.at[o - 1])
@@ -340,58 +359,53 @@
     def mate_b(ox):
         arrived(wb.at[at_x(NX - ox), other], cb_r.at[ox])
 
-    def start_of(acc, w_k):
-        k = x
+    tile_rows = 512
+
+    def multiply(acc, w_k, ox):
+        k = at_x(NX - ox)
 
         def tile(i, _):
-            r = pl.ds(pl.multiple_of(i * 256, 256), 256)
+            r = pl.ds(pl.multiple_of(i * tile_rows, tile_rows), tile_rows)
             acc[r, :] = jnp.dot(nxt[k, r, :], w_k[k], preferred_element_type=f32)
             return 0
 
-        lax.fori_loop(0, TOK // 256, tile, 0)
-
-    def rest():
+        lax.fori_loop(0, TOK // tile_rows, tile, 0)
+
+    def finish():
         ks = [at_x(NX - ox) for ox in (1, 3, 2)]
 
-        def store(i):
-            r = pl.ds(pl.multiple_of(i * 256, 256), 256)
-            return pltpu.make_async_copy(out.at[r], out_hbm.at[r], st.at[2 + i])
-
         def tile(i, _):
-            r = pl.ds(pl.multiple_of(i * 256, 256), 256)
+            r = pl.ds(pl.multiple_of(i * tile_rows, tile_rows), tile_rows)
             gate, up = gate_acc[r, :], up_acc[r, :]
             for k in ks:
                 gate += jnp.dot(nxt[k, r, :], wa_k[k], preferred_element_type=f32)
             for k in ks:
                 up += jnp.dot(nxt[k, r, :], wb_k[k], preferred_element_type=f32)
-            out[r, :] = (gate / (1.0 + jnp.exp(-gate)) * up).astype(bf16)
-            store(i).start()
+            out_ref[r, :] = (gate / (1.0 + jnp.exp(-gate)) * up).astype(bf16)
             return 0
 
-        lax.fori_loop(0, TOK // 256, tile, 0)
-        stores.extend(store(i) for i in range(TOK // 256))
+        lax.fori_loop(0, TOK // tile_rows, tile, 0)
 
     forward(1)
     forward(3)
     relay(0)
     forward(2)
-    for cp in load_nxt:
-        cp.wait()
+    pltpu.make_async_copy(nxt, nxt, ld.at[5]).wait()
     relay(1)
+    mate_a(0)
+    multiply(gate_acc, wa_k, 0)
     relay(3)
     relay(2)
     last(0)
-    mate_a(0)
-    start_of(gate_acc, wa_k)
     last(1)
     last(3)
     mate_b(0)
-    start_of(up_acc, wb_k)
+    multiply(up_acc, wb_k, 0)
     last(2)
     for ox in (1, 3, 2):
         mate_a(ox)
         mate_b(ox)
-    rest()
+    finish()
     rows64 = pl.ds(0, 15 * 64)
     bytes_of = {
         CORE: give, A1: sa, B1: sb, A2: ta, B2: tb, Z: tz.at[pl.ds(0, NZ - 1)], PW: pw.at[:, pl.ds(0, NZ - 1)],
@@ -400,22 +414,14 @@
     }
     for kind, ref in bytes_of.items():
         handle(ref, done.at[kind]).wait_send()
-    for cp in stores:
-        cp.wait()
-
-
-def keep(a_ref, b_ref, c_ref, a_out, b_out, c_out, a_buf, b_buf, c_buf, in_sem, out_sem):
-    part = TOK // 4
-    moves = [(c_ref.at[pl.ds(i * part, part)], c_buf.at[i], c_out.at[pl.ds(i * part, part)]) for i in range(4)]
-    moves += [(a_ref, a_buf, a_out), (b_ref, b_buf, b_out)]
-    reads = [pltpu.make_async_copy(s, t, in_sem.at[i]) for i, (s, t, _) in enumerate(moves)]
-    writes = [pltpu.make_async_copy(t, d, out_sem.at[i]) for i, (_, t, d) in enumerate(moves)]
-    for cp in reads:
+
+
+def keep(a_ref, b_ref, c_ref, a_out, b_out, c_out, sem):
+    moves = ((c_ref, c_out), (a_ref, a_out), (b_ref, b_out))
+    copies = [pltpu.make_async_copy(s, d, sem.at[i]) for i, (s, d) in enumerate(moves)]
+    for cp in copies:
         cp.start()
-    for r, w in zip(reads, writes):
-        r.wait()
-        w.start()
-    for cp in writes:
+    for cp in copies:
         cp.wait()
 
 
@@ -424,10 +430,10 @@
     V = pltpu.VMEM
     dma = pltpu.SemaphoreType.DMA
 
-    block = (NX, NZ, NY, ROWS, 2 * FF)
+    block = (NX, 2, NZ, NY, ROWS, FF)
     piece = (NZ, ROWS, FF)
     scratch = [
-        V((2 * NX, TOK, 256), bf16), V((TOK, 2 * FF), bf16), V((NX, TOK, 512), bf16), V((3, NZ, ROWS, 2 * FF), f32),
+        V((2 * NX, TOK, 256), bf16), V((2, TOK, FF), bf16), V((NX, TOK, 512), bf16), V((3, NZ, ROWS, 2 * FF), f32),
         V(block, f32), V(block, bf16), V(block, bf16),
         V((NX - 1, NY, *piece), bf16), V((NX, NY - 1, *piece), bf16), V((2, 2, *piece), bf16), V((NX, *piece), bf16),
         V((NY, 2, *piece), bf16), V((NX, 2, *piece), bf16),
@@ -436,9 +442,9 @@
         V((2, 128), f32), V((NZ - 1, 2, 128), f32), V((NX * NC * NY, 2, 128), f32),
         V((NZ, ROWS, 2 * FF), bf16),
         V((NX, NC, NZ, NY, ROWS, FF), bf16), V((NX, NC, NZ, NY, ROWS, FF), bf16),
-        V((TOK, FF), f32), V((TOK, FF), f32), V((2, ROWS, 2 * FF), f32), V((TOK, FF), bf16),
-        dma((2 * NX,)), dma((NX,)), dma((4,)), dma((6,)), dma((14,)),
-        dma((NX,)), dma((2,)), dma((NX,)), dma((NY,)), dma((NX,)), dma((1,)), dma((1,)), dma((1,)),
+        V((TOK, FF), f32), V((TOK, FF), f32),
+        dma((2 * NX,)), dma((6,)), dma((14,)),
+        dma((NX, 2)), dma((2,)), dma((NX,)), dma((NY,)), dma((NX,)), dma((1,)), dma((1,)), dma((1,)),
         dma((NZ - 1,)), dma((1,)), dma((1,)), dma((1,)),
         dma((NY - 1,)), dma((NX - 1,)), dma((2, NY)), dma((2, NX)), dma((NY,)), dma((NX,)), dma((NX,)), dma((NX,)),
     ]
@@ -447,26 +453,24 @@
         jax.ShapeDtypeStruct((ROWS, 2 * FF), f32),
         jax.ShapeDtypeStruct((TOK, FF), bf16),
     )
+    inputs = (tokens, grad_out, master_weight, first_moment, second_moment, next_tokens)
     results = pl.pallas_call(
         body,
         out_shape=shapes,
         in_specs=[any_] * 6,
-        out_specs=(any_,) * 3,
+        out_specs=(pl.BlockSpec(memory_space=pltpu.VMEM),) * 3,
         scratch_shapes=scratch,
         compiler_params=pltpu.CompilerParams(
-            collective_id=0, has_side_effects=True, vmem_limit_bytes=60 * 1024 * 1024
+            collective_id=0, has_side_effects=True, vmem_limit_bytes=103 * 512 * 1024
         ),
-    )(tokens, grad_out, master_weight, first_moment, second_moment, next_tokens)
+    )(*(pltpu.with_memory_space_constraint(a, pltpu.HBM) for a in inputs))
     return pl.pallas_call(
         keep,
         out_shape=shapes,
         in_specs=[any_] * 3,
         out_specs=(any_,) * 3,
-        scratch_shapes=[
-            V((ROWS, 2 * FF), f32), V((ROWS, 2 * FF), f32), V((4, TOK // 4, FF), bf16),
-            dma((6,)), dma((6,)),
-        ],
-        compiler_params=pltpu.CompilerParams(vmem_limit_bytes=60 * 1024 * 1024),
+        scratch_shapes=[dma((3,))],
+        compiler_params=pltpu.CompilerParams(vmem_limit_bytes=2 * 1024 * 1024),
     )(*results)
 
 

time: 68.6 us -> 66.4 us (0.968)
  Pallas kernels: 67.9 us -> 65.7 us
    pallas_call x1, Pallas kernels: 65.8 us -> 64.7 us  [shards(): pl.pallas_call(body, out_shape=shapes, in_specs=[any_] * 6, out_specs=(pl...]
    pallas_call x1, Pallas kernels: 2.03 us -> 1 us  [shards(): pl.pallas_call(keep, out_shape=shapes, in_specs=[any_] * 3, out_specs=(an...]
where the time goes in v4:
time: 66.4 us; the launch traced here: 66.3 us
  Pallas kernels  65.7 us (99%)
    pallas_call x1, Pallas kernels, shards(): pl.pallas_call(body, out_shape=shapes, in_specs=[any_] * 6, out_specs=(pl...  64.7 us

profile of v4, /device:TPU:1, one launch (start us, length us, event | category | flops | bytes accessed | tf_op | source)
XLA Modules:
  0.0 66.3 jit_solution(8981601788397080436)
XLA Ops:
  0.6 64.7 %shard_map.85 = (f32[8,1024]{1,0:T(8,128)S(1)}, f32[8,1024]{1,0:T(8,128)S(1)}, bf16[1024,512]{1,0:T(8,128)(2,1)S(1)}) custom-call(bf16[1024,2048]{1,0:T(8,128)(2,1)} %tok_hbm.1, bf16[1024,1024]{1,0:T(8,128)(2,1)} %cot_hbm.1, f32[8,1024]{1,0:T(8,128)} %w_hbm.1, f32[8,1024]{1,0:T(8,128)} %m_hbm.1, f32[8,1024]{1,0:T(8,128)} %v_hbm.1, bf16[1024,2048]{1,0:T(8,128)(2,1)} %nxt_hbm.1), custom_call_target="tpu_custom_call" | custom-call | tf_op jit(solution)/shard_map/pallas_call | solution.py:457
  65.3 1.0 %shard_map.86 = (f32[8,1024]{1,0:T(8,128)}, f32[8,1024]{1,0:T(8,128)}, bf16[1024,512]{1,0:T(8,128)(2,1)}) custom-call(f32[8,1024]{1,0:T(8,128)S(1)} %get-tuple-element.6.a_ref, f32[8,1024]{1,0:T(8,128)S(1)} %get-tuple-element.7.b_ref, bf16[1024,512]{1,0:T(8,128)(2,1)S(1)} %get-tuple-element.8.c_ref), custom_call_target="tpu_custom_call" | custom-call | tf_op jit(solution)/shard_map/pallas_call | solution.py:467

commit v5 on v4

--- a/solution.py
+++ b/solution.py
@@ -361,26 +361,26 @@
 
     tile_rows = 512
 
-    def multiply(acc, w_k, ox):
-        k = at_x(NX - ox)
+    tile_rows = 512
+
+    def multiply(acc, w_k, *oxs):
+        ks = [at_x(NX - ox) for ox in oxs]
 
         def tile(i, _):
             r = pl.ds(pl.multiple_of(i * tile_rows, tile_rows), tile_rows)
-            acc[r, :] = jnp.dot(nxt[k, r, :], w_k[k], preferred_element_type=f32)
+            terms = [jnp.dot(nxt[k, r, :], w_k[k], preferred_element_type=f32) for k in ks]
+            acc[r, :] = sum(terms[1:], terms[0]) if 0 in oxs else sum(terms, acc[r, :])
             return 0
 
         lax.fori_loop(0, TOK // tile_rows, tile, 0)
 
     def finish():
-        ks = [at_x(NX - ox) for ox in (1, 3, 2)]
+        k = at_x(NX - 2)
 
         def tile(i, _):
             r = pl.ds(pl.multiple_of(i * tile_rows, tile_rows), tile_rows)
-            gate, up = gate_acc[r, :], up_acc[r, :]
-            for k in ks:
-                gate += jnp.dot(nxt[k, r, :], wa_k[k], preferred_element_type=f32)
-            for k in ks:
-                up += jnp.dot(nxt[k, r, :], wb_k[k], preferred_element_type=f32)
+            gate = gate_acc[r, :] + jnp.dot(nxt[k, r, :], wa_k[k], preferred_element_type=f32)
+            up = up_acc[r, :] + jnp.dot(nxt[k, r, :], wb_k[k], preferred_element_type=f32)
             out_ref[r, :] = (gate / (1.0 + jnp.exp(-gate)) * up).astype(bf16)
             return 0
 
@@ -398,13 +398,18 @@
     relay(2)
     last(0)
     last(1)
-    last(3)
     mate_b(0)
     multiply(up_acc, wb_k, 0)
+    last(3)
+    mate_a(1)
+    mate_a(3)
+    multiply(gate_acc, wa_k, 1, 3)
     last(2)
-    for ox in (1, 3, 2):
-        mate_a(ox)
-        mate_b(ox)
+    mate_b(1)
+    mate_b(3)
+    multiply(up_acc, wb_k, 1, 3)
+    mate_a(2)
+    mate_b(2)
     finish()
     rows64 = pl.ds(0, 15 * 64)
     bytes_of = {

time: 66.4 us -> 65.1 us (0.980)
  Pallas kernels: 65.7 us -> 64.4 us
    pallas_call x1, Pallas kernels: 64.7 us -> 63.4 us  [shards(): pl.pallas_call(body, out_shape=shapes, in_specs=[any_] * 6, out_specs=(pl...]
where the time goes in v5:
time: 65.1 us; the launch traced here: 65 us
  Pallas kernels  64.4 us (99%)
    pallas_call x1, Pallas kernels, shards(): pl.pallas_call(body, out_shape=shapes, in_specs=[any_] * 6, out_specs=(pl...  63.4 us

profile of v5, /device:TPU:1, one launch (start us, length us, event | category | flops | bytes accessed | tf_op | source)
XLA Modules:
  0.0 65.0 jit_solution(10405043963210633227)
XLA Ops:
  0.6 63.4 %shard_map.85 = (f32[8,1024]{1,0:T(8,128)S(1)}, f32[8,1024]{1,0:T(8,128)S(1)}, bf16[1024,512]{1,0:T(8,128)(2,1)S(1)}) custom-call(bf16[1024,2048]{1,0:T(8,128)(2,1)} %tok_hbm.1, bf16[1024,1024]{1,0:T(8,128)(2,1)} %cot_hbm.1, f32[8,1024]{1,0:T(8,128)} %w_hbm.1, f32[8,1024]{1,0:T(8,128)} %m_hbm.1, f32[8,1024]{1,0:T(8,128)} %v_hbm.1, bf16[1024,2048]{1,0:T(8,128)(2,1)} %nxt_hbm.1), custom_call_target="tpu_custom_call" | custom-call | tf_op jit(solution)/shard_map/pallas_call | solution.py:462
  64.0 1.0 %shard_map.86 = (f32[8,1024]{1,0:T(8,128)}, f32[8,1024]{1,0:T(8,128)}, bf16[1024,512]{1,0:T(8,128)(2,1)}) custom-call(f32[8,1024]{1,0:T(8,128)S(1)} %get-tuple-element.6.a_ref, f32[8,1024]{1,0:T(8,128)S(1)} %get-tuple-element.7.b_ref, bf16[1024,512]{1,0:T(8,128)(2,1)S(1)} %get-tuple-element.8.c_ref), custom_call_target="tpu_custom_call" | custom-call | tf_op jit(solution)/shard_map/pallas_call | solution.py:472

commit v6 on v5

--- a/solution.py
+++ b/solution.py
@@ -57,7 +57,9 @@
     def in_plane(ox, oc, oy):
         return {"x": at_x(ox), "c": other if oc else c, "y": at_y(oy)}
 
-    CORE, A1, B1, A2, B2, Z, PW, QZ, Q, G, GA, GB, CA, CB = range(14)
+    CORE = A1 = B1 = A2 = B2 = 0
+    Z = PW = G = GA = GB = CA = 1
+    CB, QZ, Q = 2, 3, 4
 
     def send(src, dst, kind, rs, to):
         pltpu.make_async_remote_copy(
@@ -141,8 +143,7 @@
             for k in via_prev:
                 near_a(1, k, gate_sum(1, k))
         if j == 2:
-            for k in via_next:
-                near_a(2, k, gate_sum(2, k))
+            near_a(2, 2, gate_sum(2, 2))
 
     def combine_up(j):
         arrived(take.at[j, 1], core_r.at[j, 1])
@@ -204,6 +205,8 @@
         if j:
             combine_gate(j - 1)
             combine_up(j - 1)
+        if j == NX - 1:
+            add_b(0)
         load_tok[2 * j + 1].wait()
         lhs = rows_of(2 * j + 1)
         own[j, 0] = block_grad(lhs, 0)
@@ -215,23 +218,23 @@
             pass_on(0, 7, 7)
             pass_on(0, 4, 4)
     combine_gate(NX - 1)
+    add_b(1)
+    add_a(0)
+    add_a(1)
+    near_a(2, 0, gate_sum(2, 0))
+    add_b(2)
     combine_up(NX - 1)
     for cp in load_nxt:
         cp.start()
-    add_a(0)
-    add_b(0)
-    add_a(1)
-    add_b(1)
-    add_b(2)
-    add_b(3)
     arrived(pw.at[:, at_z(7)], pw_r.at[0])
     pass_on(1, 2, 1)
     arrived(pw.at[:, at_z(1)], pw_r.at[6])
     pass_on(7, 6, 7)
     second_b(0)
     second_a(2)
+    add_b(3)
+    second_b(1)
     second_a(1)
-    second_b(1)
     second_b(2)
     second_a(3)
     total = second_a(0)
@@ -411,14 +414,14 @@
     mate_a(2)
     mate_b(2)
     finish()
-    rows64 = pl.ds(0, 15 * 64)
-    bytes_of = {
-        CORE: give, A1: sa, B1: sb, A2: ta, B2: tb, Z: tz.at[pl.ds(0, NZ - 1)], PW: pw.at[:, pl.ds(0, NZ - 1)],
-        QZ: rsqz, Q: rsq.at[pl.ds(1, len(plane))], G: gz.at[pl.ds(1, NZ - 1)],
-        GA: wa.reshape(D, FF).at[rows64], GB: wb.reshape(D, FF).at[rows64], CA: wa.at[:, c], CB: wb.at[:, c],
-    }
-    for kind, ref in bytes_of.items():
-        handle(ref, done.at[kind]).wait_send()
+    kib = nxt.reshape(NX * TOK, 512)
+    piece = NZ * ROWS
+    reduced = 2048 + (12 + 12 + 3 + 3) * piece
+    rest = (2 * 16 + 96) * (NZ - 1) + (15 + 15 + 16) * piece
+    for kind, n in enumerate((reduced, rest, 16 * piece)):
+        handle(kib.at[pl.ds(0, n)], done.at[kind]).wait_send()
+    handle(rsqz, done.at[QZ]).wait_send()
+    handle(rsq.at[pl.ds(1, len(plane))], done.at[Q]).wait_send()
 
 
 def keep(a_ref, b_ref, c_ref, a_out, b_out, c_out, sem):
@@ -448,7 +451,7 @@
         V((NZ, ROWS, 2 * FF), bf16),
         V((NX, NC, NZ, NY, ROWS, FF), bf16), V((NX, NC, NZ, NY, ROWS, FF), bf16),
         V((TOK, FF), f32), V((TOK, FF), f32),
-        dma((2 * NX,)), dma((6,)), dma((14,)),
+        dma((2 * NX,)), dma((6,)), dma((5,)),
         dma((NX, 2)), dma((2,)), dma((NX,)), dma((NY,)), dma((NX,)), dma((1,)), dma((1,)), dma((1,)),
         dma((NZ - 1,)), dma((1,)), dma((1,)), dma((1,)),
         dma((NY - 1,)), dma((NX - 1,)), dma((2, NY)), dma((2, NX)), dma((NY,)), dma((NX,)), dma((NX,)), dma((NX,)),

time: 65.1 us -> 64.7 us (level)
  no operation moved by 1% of the time
where the time goes in v6:
time: 64.7 us; the launch traced here: 64.6 us
  Pallas kernels  64 us (99%)
    pallas_call x1, Pallas kernels, shards(): pl.pallas_call(body, out_shape=shapes, in_specs=[any_] * 6, out_specs=(pl...  63 us

profile of v6, /device:TPU:1, one launch (start us, length us, event | category | flops | bytes accessed | tf_op | source)
XLA Modules:
  0.0 64.6 jit_solution(14436715809250859391)
XLA Ops:
  0.6 63.0 %shard_map.85 = (f32[8,1024]{1,0:T(8,128)S(1)}, f32[8,1024]{1,0:T(8,128)S(1)}, bf16[1024,512]{1,0:T(8,128)(2,1)S(1)}) custom-call(bf16[1024,2048]{1,0:T(8,128)(2,1)} %tok_hbm.1, bf16[1024,1024]{1,0:T(8,128)(2,1)} %cot_hbm.1, f32[8,1024]{1,0:T(8,128)} %w_hbm.1, f32[8,1024]{1,0:T(8,128)} %m_hbm.1, f32[8,1024]{1,0:T(8,128)} %v_hbm.1, bf16[1024,2048]{1,0:T(8,128)(2,1)} %nxt_hbm.1), custom_call_target="tpu_custom_call" | custom-call | tf_op jit(solution)/shard_map/pallas_call | solution.py:465
  63.6 1.0 %shard_map.86 = (f32[8,1024]{1,0:T(8,128)}, f32[8,1024]{1,0:T(8,128)}, bf16[1024,512]{1,0:T(8,128)(2,1)}) custom-call(f32[8,1024]{1,0:T(8,128)S(1)} %get-tuple-element.6.a_ref, f32[8,1024]{1,0:T(8,128)S(1)} %get-tuple-element.7.b_ref, bf16[1024,512]{1,0:T(8,128)(2,1)S(1)} %get-tuple-element.8.c_ref), custom_call_target="tpu_custom_call" | custom-call | tf_op jit(solution)/shard_map/pallas_call | solution.py:475

commit v7 on v6

--- a/solution.py
+++ b/solution.py
@@ -292,13 +292,17 @@
         clipped = jnp.concatenate([g[:, :FF] * gate_factor, g[:, FF:] * up_factor], axis=1)
         return 0.9 * pw[1, slot] + 0.1 * clipped, 0.95 * pw[2, slot] + 0.05 * clipped * clipped
 
-    for o in range(NZ):
-        k = at_z(NZ - o)
-        first, second = moments(gz[o].astype(f32), k)
-        low = pw[0, k] * (1.0 - 0.003 * 0.1) - (first * first_scale) / (jnp.sqrt(second * second_scale) + 1e-08)
-        low = low.astype(bf16)
-        wa[x, c, k, y] = low[:, :FF]
-        wb[x, c, k, y] = low[:, FF:]
+    def low_rows(dst, h, scale):
+        cols = pl.ds(h * FF, FF)
+        for o in range(NZ):
+            k = at_z(NZ - o)
+            clipped = gz[o, :, cols].astype(f32) * scale
+            first = 0.9 * pw[1, k, :, cols] + 0.1 * clipped
+            second = 0.95 * pw[2, k, :, cols] + 0.05 * clipped * clipped
+            low = pw[0, k, :, cols] * (1.0 - 0.003 * 0.1) - (first * first_scale) / (
+                jnp.sqrt(second * second_scale) + 1e-08
+            )
+            dst[x, c, k, y] = low.astype(bf16)
 
     def pa(ox, oy, lo=0, n=NZ):
         return wa.at[at_x(NX - ox), c, pl.ds(lo, n), at_y(NY - oy)]
@@ -322,10 +326,13 @@
             send(pb(ox, 0), pb(ox, 0), GB, nb_r.at[i, ox], yp(o))
         to_mate_b(ox, 0)
 
+    low_rows(wa, 0, gate_factor)
     for o in (1, 3, 2):
         send(pa(0, 0), pa(0, 0), GA, ga_r.at[o - 1], yp(o))
+    spread_a(0)
+    low_rows(wb, 1, up_factor)
+    for o in (1, 3, 2):
         send(pb(0, 0), pb(0, 0), GB, gb_r.at[o - 1], xp(o))
-    spread_a(0)
     spread_b(0)
 
     first, second = moments(grad, z)

time: 64.7 us -> 65.8 us (1.017)
  Pallas kernels: 64 us -> 65.1 us
    pallas_call x1, Pallas kernels: 63 us -> 64.1 us  [shards(): pl.pallas_call(body, out_shape=shapes, in_specs=[any_] * 6, out_specs=(pl...]
where the time goes in v7:
time: 65.8 us
  Pallas kernels  65.1 us (99%)
    pallas_call x1, Pallas kernels, shards(): pl.pallas_call(body, out_shape=shapes, in_specs=[any_] * 6, out_specs=(pl...  64.1 us

profile of v7, /device:TPU:1, one launch (start us, length us, event | category | flops | bytes accessed | tf_op | source)
XLA Modules:
  0.0 65.8 jit_solution(4127338901573636749)
XLA Ops:
  0.6 64.1 %shard_map.85 = (f32[8,1024]{1,0:T(8,128)S(1)}, f32[8,1024]{1,0:T(8,128)S(1)}, bf16[1024,512]{1,0:T(8,128)(2,1)S(1)}) custom-call(bf16[1024,2048]{1,0:T(8,128)(2,1)} %tok_hbm.1, bf16[1024,1024]{1,0:T(8,128)(2,1)} %cot_hbm.1, f32[8,1024]{1,0:T(8,128)} %w_hbm.1, f32[8,1024]{1,0:T(8,128)} %m_hbm.1, f32[8,1024]{1,0:T(8,128)} %v_hbm.1, bf16[1024,2048]{1,0:T(8,128)(2,1)} %nxt_hbm.1), custom_call_target="tpu_custom_call" | custom-call | tf_op jit(solution)/shard_map/pallas_call | solution.py:472
  64.8 1.0 %shard_map.86 = (f32[8,1024]{1,0:T(8,128)}, f32[8,1024]{1,0:T(8,128)}, bf16[1024,512]{1,0:T(8,128)(2,1)}) custom-call(f32[8,1024]{1,0:T(8,128)S(1)} %get-tuple-element.6.a_ref, f32[8,1024]{1,0:T(8,128)S(1)} %get-tuple-element.7.b_ref, bf16[1024,512]{1,0:T(8,128)(2,1)S(1)} %get-tuple-element.8.c_ref), custom_call_target="tpu_custom_call" | custom-call | tf_op jit(solution)/shard_map/pallas_call | solution.py:482
